TPU v7x, 256 devices: a whole 4x4x8 slice. The times are simulated.
256 devices in a mesh: row: 16 (over x_hi, z), blk: 16 (over x_lo, y, core).
Axes of the slice: x: 4 (x_hi: 2, x_lo: 2; x = x_hi * 2 + x_lo), y: 4, z: 8, core: 2. Of those that a mesh axis runs over, the one named last changes fastest.
Arguments:
- source_table: bfloat16 [8192, 512], P('blk'), may hold values from -6 to 6
- target_table: bfloat16 [131072, 512], P(('row', 'blk')), may hold values from -6 to 6
- message_weight: bfloat16 [512, 512], replicated, may hold values from -0.25 to 0.25
- self_weight: bfloat16 [512, 512], replicated, may hold values from -0.25 to 0.25
- tile_lists: int32 [256, 16], P(('row', 'blk')), may hold values from 0 to 15, each once within a row
- key_offsets: int32 [131072, 16], P(('row', 'blk')), may hold values from 0 to 511
- list_lengths: int32 [256], P(('row', 'blk')), may hold values from 1 to 16, 2048 in all
- cotangent: bfloat16 [131072, 512], P(('row', 'blk')), may hold values from -6 to 6
Outputs:
- updated: bfloat16 [131072, 512], P(('row', 'blk'))
- target_gradient: bfloat16 [131072, 512], P(('row', 'blk'))
- source_gradient: bfloat16 [8192, 512], P(('blk', 'row'))
- self_gradient: float32 [512, 512], replicated
- message_gradient: float32 [512, 512], replicated
Inputs may be any that keep to these rules, and one draw needn't show every extreme that they name: Each row of tile_lists names every one of the 16 source tiles once. A target tile uses the first list_lengths entries of its row of tile_lists.
All inputs are finite; a program needn't handle non-finite values. No bound on the sum of `list_lengths` on one device may be relied on, other than what follows from the above.
Results may differ from a plain program's by a relative error of at most 0.0058.
Values may be sent and summed in bfloat16 or wider, within the bound.
A program may use at most 64 MiB of HBM per device.

v0:
```python
import jax
import jax.numpy as jnp
from jax import lax
from jax.sharding import PartitionSpec as P


def slot_table(lists):
    slot_count = lists.shape[1]
    slot_ids = lax.iota(jnp.int32, slot_count)
    matches = lists[:, :, None] == slot_ids[None, None, :]
    return jnp.sum(jnp.where(matches, slot_ids[None, :, None], 0), axis=1)


def tile_patterns(offset_tiles, slot_column, lengths, tile_rows):
    slot_count = offset_tiles.shape[2]
    chosen_slot = lax.iota(jnp.int32, slot_count)[None, None, :] == slot_column[:, None, None]
    chosen = jnp.sum(jnp.where(chosen_slot, offset_tiles, 0), axis=2)
    used = slot_column < lengths
    positions = lax.iota(jnp.int32, tile_rows)
    pattern = (chosen[:, :, None] == positions[None, None, :]) & used[:, None, None]
    return pattern.astype(jnp.bfloat16)


def local(
    source_table,
    target_table,
    message_weight,
    self_weight,
    tile_lists,
    key_offsets,
    list_lengths,
    cotangent,
):
    tile_rows = target_table.shape[0] // tile_lists.shape[0]
    tiles_here = tile_lists.shape[0]
    slot_count = tile_lists.shape[1]
    width = target_table.shape[1]
    block_rows = source_table.shape[0]
    row_devices = lax.axis_size("row")
    share_rows = block_rows // row_devices
    own_rows = lax.dynamic_slice_in_dim(
        source_table, lax.axis_index("row") * share_rows, share_rows, 0
    )
    projected = jnp.dot(source_table, message_weight, preferred_element_type=jnp.float32).astype(
        jnp.bfloat16
    )
    inverse_tile = 1.0 / list_lengths.astype(jnp.float32)
    slot_of = slot_table(tile_lists)
    offset_tiles = key_offsets.reshape(tiles_here, tile_rows, slot_count)
    start_sum = jnp.zeros((target_table.shape[0], width), jnp.float32)
    pieces = lax.all_gather(projected, "blk", axis=0, tiled=True)
    piece_tiles = pieces.shape[0] // tile_rows

    def gather_visit(local_tile, running):
        source_tile = lax.dynamic_slice_in_dim(pieces, local_tile * tile_rows, tile_rows, 0)
        slot_column = lax.dynamic_index_in_dim(slot_of, local_tile, 1, keepdims=False)
        pattern = tile_patterns(offset_tiles, slot_column, list_lengths, tile_rows)
        added = jnp.einsum("trc,cw->trw", pattern, source_tile, preferred_element_type=jnp.float32)
        return running + added.reshape(running.shape)

    gathered = lax.fori_loop(0, piece_tiles, gather_visit, start_sum)
    inverse_row = jnp.repeat(inverse_tile, tile_rows)[:, None]
    preact = (
        jnp.dot(target_table, self_weight, preferred_element_type=jnp.float32)
        + gathered * inverse_row
    )
    sigmoid_pre = jax.nn.sigmoid(preact)
    updated = (target_table.astype(jnp.float32) + preact * sigmoid_pre).astype(jnp.bfloat16)
    upstream = cotangent.astype(jnp.float32)
    grad_pre = (upstream * sigmoid_pre * (1.0 + preact * (1.0 - sigmoid_pre))).astype(jnp.bfloat16)
    target_gradient = (
        upstream + jnp.dot(grad_pre, self_weight.T, preferred_element_type=jnp.float32)
    ).astype(jnp.bfloat16)
    grad_tiles = grad_pre.reshape(tiles_here, tile_rows, width)

    def tile_terms(slot_column, offsets, lengths, inverses, grads):
        pattern = tile_patterns(offsets, slot_column, lengths, tile_rows)
        terms = jnp.einsum("trc,trw->tcw", pattern, grads, preferred_element_type=jnp.float32)
        return jnp.sum(terms * inverses[:, None, None], axis=0)

    def partial_visit(local_tile, running):
        slot_column = lax.dynamic_index_in_dim(slot_of, local_tile, 1, keepdims=False)
        term = tile_terms(slot_column, offset_tiles, list_lengths, inverse_tile, grad_tiles)
        return lax.dynamic_update_slice_in_dim(running, term, local_tile * tile_rows, 0)

    block_sum = lax.psum_scatter(
        lax.fori_loop(
            0,
            block_rows * lax.axis_size("blk") // tile_rows,
            partial_visit,
            jnp.zeros((block_rows * lax.axis_size("blk"), width), jnp.float32),
        ),
        "blk",
        scatter_dimension=0,
        tiled=True,
    )
    source_sum = lax.psum_scatter(block_sum, "row", scatter_dimension=0, tiled=True)
    source_grad_rounded = source_sum.astype(jnp.bfloat16)
    source_gradient = jnp.dot(
        source_grad_rounded, message_weight.T, preferred_element_type=jnp.float32
    ).astype(jnp.bfloat16)
    self_partial = jnp.dot(target_table.T, grad_pre, preferred_element_type=jnp.float32)
    message_partial = jnp.dot(own_rows.T, source_grad_rounded, preferred_element_type=jnp.float32)
    self_total, message_total = lax.psum((self_partial, message_partial), ("row", "blk"))
    target_total = target_table.shape[0] * row_devices * lax.axis_size("blk")
    source_total = block_rows * lax.axis_size("blk")
    self_gradient = self_total * target_total ** (-0.5)
    message_gradient = message_total * source_total ** (-0.5)
    return (updated, target_gradient, source_gradient, self_gradient, message_gradient)


def solution(mesh):
    placed = (
        P("blk", None),
        P(("row", "blk"), None),
        P(),
        P(),
        P(("row", "blk"), None),
        P(("row", "blk"), None),
        P(("row", "blk")),
        P(("row", "blk"), None),
    )
    return jax.shard_map(
        local,
        mesh=mesh,
        in_specs=placed,
        out_specs=(
            P(("row", "blk"), None),
            P(("row", "blk"), None),
            P(("blk", "row"), None),
            P(),
            P(),
        ),
        check_vma=False,
    )
```

profile of v0, /device:TPU:1, one launch (start us, length us, event | category | flops | bytes accessed | tf_op | source)
XLA Modules:
  0.0 807.1 jit_solution(3190670035176118978)
XLA Ops:
  7.2 2.5 convolution_convert_fusion
  11.2 58.1 %all-gather.2.cloned.1.call-done = bf16[8192,512]{1,0:T(8,128)(2,1)} async-done(((bf16[512,512]{1,0:T(8,128)(2,1)}), bf16[8192,512]{1,0:T(8,128)(2,1)}) %all-gather.2.cloned.1.call-update) | async-done | bytes 8388624 | tf_op jit(solution)/shard_map/all_gather | solution.py:51
  69.3 80.6 %while.28 = (s32[]{:T(128)}, f32[512,512]{1,0:T(8,128)S(1)}, s32[1,16]{1,0:T(1,128)S(1)}, s32[1,512,16]{1,2,0:T(8,128)}, s32[1]{0:T(128)}, /*index=5*/bf16[8192,...) while((s32[]{:T(128)}, f32[512,512]{1,0:T(8,128)S(1)}, s32[1,16]{1,0:T(1,128)S(1)}, ...), condition=%wide.region_3.4_spmd.clone, body=%wide.region_1.3_spmd.clone.sunk | while | flops 269499936 | bytes 2659034 | solution.py:61
  72.7 1.6 convolution_add_fusion.4
  77.8 1.6 convolution_add_fusion.4
  82.8 1.6 convolution_add_fusion.4
  87.9 1.6 convolution_add_fusion.4
  92.9 1.6 convolution_add_fusion.4
  97.9 1.6 convolution_add_fusion.4
  103.0 1.6 convolution_add_fusion.4
  108.0 1.6 convolution_add_fusion.4
  113.1 1.6 convolution_add_fusion.4
  118.1 1.6 convolution_add_fusion.4
  123.2 1.6 convolution_add_fusion.4
  128.2 1.6 convolution_add_fusion.4
  133.2 1.6 convolution_add_fusion.4
  138.3 1.6 convolution_add_fusion.4
  143.3 1.6 convolution_add_fusion.4
  148.4 1.6 convolution_add_fusion.4
  150.0 3.0 fusion.15
  153.0 7.9 broadcast_in_dim.94
  160.9 67.2 %while.27 = (s32[]{:T(128)}, f32[8192,512]{1,0:T(8,128)}, s32[1,16]{1,0:T(1,128)S(1)}, s32[1,512,16]{1,2,0:T(8,128)S(1)}, s32[1]{0:T(128)}, /*index=5*/bf16[1,51...) while((s32[]{:T(128)}, f32[8192,512]{1,0:T(8,128)}, ...), condition=%wide.region_6.7_spmd, body=%wide.region_4.6_spmd.sunk | while | flops 269237792 | bytes 1610968 | solution.py:87
  163.6 1.5 fusion.37
  167.8 1.6 fusion.37
  172.0 1.6 fusion.37
  176.2 1.6 fusion.37
  180.3 1.6 fusion.37
  184.5 1.6 fusion.37
  188.7 1.6 fusion.37
  192.9 1.6 fusion.37
  197.1 1.6 fusion.37
  201.4 1.5 fusion.37
  205.5 1.6 fusion.37
  209.7 1.6 fusion.37
  213.9 1.6 fusion.37
  218.2 1.5 fusion.37
  222.3 1.6 fusion.37
  226.5 1.6 fusion.37
  228.2 100.0 %reduce-scatter.3.cloned.1.call-done = f32[512,512]{1,0:T(8,128)} async-done(((f32[8192,512]{1,0:T(8,128)}), f32[512,512]{1,0:T(8,128)}) %reduce-scatter.3.cloned.1.call-update) | async-done | bytes 1048592 | tf_op jit(solution)/shard_map/reduce_scatter | solution.py:86
  328.3 1.4 convolution_bitcast_fusion
  329.7 196.7 %reduce-scatter.5.cloned.1.call-done = f32[32,512]{1,0:T(8,128)} async-done(((f32[512,512]{1,0:T(8,128)}), f32[32,512]{1,0:T(8,128)}) %reduce-scatter.5.cloned.1.call-update) | async-done | bytes 65552 | tf_op jit(solution)/shard_map/reduce_scatter | solution.py:97
  526.4 2.1 fusion.16
  528.6 1.3 fusion.13
  529.9 1.7 convolution_convert_fusion.1
  531.6 264.0 %all-reduce.3.cloned.1.call-done = (f32[512,512]{0,1:T(8,128)}, f32[512,512]{1,0:T(8,128)}) async-done(((f32[512,512]{0,1:T(8,128)}, f32[512,512]{1,0:T(8,128)}), (f32[512,512]{0,1:T(8,128)}, f32[512,512]{1,0:T(8,128)})) %all-reduce.3.cloned.1.call-update) | async-done | bytes 2097168 | tf_op jit(solution)/shard_map/psum | solution.py:104
  795.6 1.3 broadcast_multiply_fusion.1
  797.0 1.3 copy.15
  798.3 2.3 broadcast_multiply_fusion
  (116 shorter events, 55.4 us)
Async XLA Ops:
  7.2 142.8 %copy-start = (bf16[512,512]{1,0:T(8,128)(2,1)S(1)}, bf16[512,512]{1,0:T(8,128)(2,1)}, u32[]{:S(2)}) copy-start(bf16[512,512]{1,0:T(8,128)(2,1)} %param.15) | copy-start | bytes 1572868
  7.2 62.2 %all-gather.2.cloned.1.call-start = ((), (), s32[]{:S(2)}) async-start(), calls=%async_computation.2 | async-start | bytes 8912896 | tf_op jit(solution)/shard_map/all_gather | solution.py:51
  9.7 318.5 %reduce-scatter.3.cloned.1.call-start = ((), (), s32[]{:S(2)}) async-start(), calls=%async_computation.3 | async-start | bytes 17825792 | tf_op jit(solution)/shard_map/reduce_scatter | solution.py:86
  150.0 10.9 %copy-start.1 = (s32[1,512,16]{1,2,0:T(8,128)S(1)}, s32[1,512,16]{1,2,0:T(8,128)}, u32[]{:S(2)}) copy-start(s32[1,512,16]{1,2,0:T(8,128)} %get-tuple-element.461) | copy-start | bytes 98308
  160.9 167.4 %copy-start.3 = (bf16[512,512]{1,0:T(8,128)(2,1)S(1)}, bf16[512,512]{1,0:T(8,128)(2,1)}, u32[]{:S(2)}) copy-start(bf16[512,512]{1,0:T(8,128)(2,1)} %param.13) | copy-start | bytes 1572868
  160.9 367.7 %copy-start.4 = (bf16[512,512]{1,0:T(8,128)(2,1)S(1)}, bf16[512,512]{1,0:T(8,128)(2,1)}, u32[]{:S(2)}) copy-start(bf16[512,512]{1,0:T(8,128)(2,1)} %param.19) | copy-start | bytes 1572868
  160.9 369.0 %copy-start.2 = (bf16[512,512]{1,0:T(8,128)(2,1)S(1)}, bf16[512,512]{1,0:T(8,128)(2,1)}, u32[]{:S(2)}) copy-start(bf16[512,512]{1,0:T(8,128)(2,1)} %param.14) | copy-start | bytes 1572868
  228.1 298.3 %reduce-scatter.5.cloned.1.call-start = ((), (), s32[]{:S(2)}) async-start(), calls=%async_computation.4 | async-start | bytes 1114112 | tf_op jit(solution)/shard_map/reduce_scatter | solution.py:97
  328.2 467.4 %all-reduce.3.cloned.1.call-start = ((), (), s32[]{:S(2)}) async-start(), calls=%async_computation.5 | async-start | bytes 4194304 | tf_op jit(solution)/shard_map/psum | solution.py:104
Sparse Core Ops, SparseCore 0:
  10.4 58.8 all-gather.1
  228.2 99.9 reduce-scatter.2
  332.0 194.3 reduce-scatter.4
  532.4 263.1 all-reduce.2
where the time goes:
time: 811 us; the launch traced here: 807 us
  waiting for transfers between devices  619 us (76%)
  matrix products  63 us (8%)
  loops' own time  42.4 us (5%)
  other arithmetic  40.2 us (5%)
  local copies, waits for them, and re-layouts  27.9 us (3%)
  between operations  14.5 us (2%)
    psum x1, waiting for transfers between devices, local(): lax.psum((self_partial, message_partial), ('row', 'blk'))  264 us
    reduce_scatter x1, waiting for transfers between devices, local(): lax.psum_scatter(block_sum, 'row', scatter_dimension=0, tiled=True)  197 us
    reduce_scatter x1, waiting for transfers between devices, local(): lax.psum_scatter(lax.fori_loop(0, block_rows * lax.axis_size('blk') // ti...  100 us
    all_gather x1, waiting for transfers between devices, local(): pieces = lax.all_gather(projected, 'blk', axis=0, tiled=True)  58.1 us
    dot_general x16, matrix products, gather_visit(): jnp.einsum('trc,cw->trw', pattern, source_tile, preferred_element_type=jn...  25.9 us
    dot_general x16, matrix products, tile_terms(): jnp.einsum('trc,trw->tcw', pattern, grads, preferred_element_type=jnp.flo...  25.1 us
    another operation x1, loops' own time, local(): gathered = lax.fori_loop(0, piece_tiles, gather_visit, start_sum)  21.4 us
    another operation x1, loops' own time, local(): lax.fori_loop(0, block_rows * lax.axis_size('blk') // tile_rows, partial_...  21 us
  transfers between devices with their start and end apart: 4, of which 4 were waited for; matrix products, arithmetic and copies ran while one was open for 1% of the time, Pallas kernels for 0%

commit v1 on v0

v1 whole, which is shorter than its diff:
```python
import functools

import jax
import jax.numpy as jnp
from jax import lax
from jax.experimental import pallas as pl
from jax.experimental.pallas import tpu as pltpu
from jax.sharding import PartitionSpec as P

XN, YN, ZN = 4, 4, 8
HALF = 256
EXTRA = 16
F32 = jnp.float32
BF16 = jnp.bfloat16


def dot(a, b, ca=1, cb=0):
    return lax.dot_general(a, b, (((ca,), (cb,)), ((), ())), preferred_element_type=F32)


def slot(col, dy, core):
    return col * 8 + dy * 2 + core


def kernel(
    s_hbm, t_hbm, wm_hbm, ws_hbm, lists_ref, ko_ref, len_ref, cot_hbm,
    upd_hbm, tg_hbm, sg_ref, w_out,
    sbuf, gbuf, tv, cotv, wmv, wsv, acc, base, bbuf, updv, tgv, koff,
    give, got, wsend, wrecv, zbuf, wres, rsend, rrecv,
    lsem, ssend1, srecv1, ssend2, srecv2, gsem, wssem, wrsem, zssem, zrsem, assem, arsem, bssem, brsem, rssem, rrsem,
):
    r = lax.axis_index("row")
    b = lax.axis_index("blk")
    x = lax.div(r, 8) * 2 + lax.div(b, 8)
    y = lax.rem(lax.div(b, 2), 4)
    z = lax.rem(r, 8)
    c = lax.rem(b, 2)

    def dev(dx=0, dy=0, dz=0, flip=False):
        xx = lax.rem(x + dx, XN)
        yy = lax.rem(y + dy, YN)
        zz = lax.rem(z + dz, ZN)
        cc = 1 - c if flip else c
        return {"row": lax.div(xx, 2) * 8 + zz, "blk": lax.rem(xx, 2) * 8 + yy * 2 + cc}

    def remote(src, dst, ss, rs, to):
        return pltpu.make_async_remote_copy(
            src_ref=src, dst_ref=dst, send_sem=ss, recv_sem=rs,
            device_id=to, device_id_type=pl.DeviceIdType.MESH,
        )

    loads = {}
    for i, (name, src, dst) in enumerate((
        ("s", s_hbm, sbuf.at[0]), ("t", t_hbm, tv), ("ws", ws_hbm, wsv), ("wm", wm_hbm, wmv), ("cot", cot_hbm, cotv),
    )):
        loads[name] = pltpu.make_async_copy(src, dst, lsem.at[i])
        loads[name].start()

    plane = [(dx, dy) for dx in range(XN) for dy in range(YN) if (dx, dy) != (0, 0)]
    rows = [(dxh, dz) for dxh in range(2) for dz in range(ZN) if (dxh, dz) != (0, 0)]
    barrier = pltpu.get_barrier_semaphore()
    partners = [dev(flip=True)] + [dev(dx, dy) for dx, dy in plane] + [
        dev(2 * dxh, 0, dz) for dxh, dz in rows if (dxh, dz) != (1, 0)
    ]
    for to in partners:
        pl.semaphore_signal(barrier, inc=1, device_id=to, device_id_type=pl.DeviceIdType.MESH)
    pl.semaphore_wait(barrier, len(partners))

    sends = []

    class Gather:
        def __init__(self, buf, ssem, rsem):
            self.buf, self.ssem, self.rsem, self.n = buf, ssem, rsem, 0

        def send(self, t, h, to_t, to):
            cp = remote(
                self.buf.at[t, h], self.buf.at[to_t, h], self.ssem.at[self.n], self.rsem.at[to_t * 2 + h], to
            )
            cp.start()
            self.n += 1
            sends.append(cp)

        def start(self, h):
            t = slot(0, 0, 0)
            first = (1, 3) if h == 0 else (3, 1)
            for dy in first:
                self.send(t, h, slot(0, (4 - dy) % 4, 0), dev(0, dy))
            self.send(t, h, slot(1, 0, 0), dev(1 if h == 0 else 3, 0))
            self.send(t, h, slot(0, 0, 1), dev(flip=True))

        def wait(self, col, dy, core, h):
            t = slot(col, dy, core)
            remote(
                self.buf.at[t, h], self.buf.at[t, h], self.ssem.at[0], self.rsem.at[t * 2 + h], dev(flip=True)
            ).wait_recv()

        def take(self, col, dy, h):
            self.wait(col, dy, 0, h)
            t = slot(col, dy, 0)
            if col == 0:
                if (dy, h) == (3, 0):
                    self.send(t, h, slot(0, 2, 0), dev(0, 1))
                if (dy, h) == (1, 1):
                    self.send(t, h, slot(0, 2, 0), dev(0, 3))
                self.send(t, h, slot(1, dy, 0), dev(1 if h == 0 else 3, 0))
            self.send(t, h, slot(col, dy, 1), dev(flip=True))

    first = Gather(sbuf, ssend1, srecv1)
    loads["s"].wait()
    first.start(0)
    first.start(1)

    k_row = lax.broadcasted_iota(jnp.int32, (16, 16), 0)
    s_col = lax.broadcasted_iota(jnp.int32, (16, 16), 1)
    kc, kd, ke = k_row // 8, (k_row // 2) % 4, k_row % 2
    xl = lax.rem(x, 2)
    tile_id = ((xl + kc) % 2) * 8 + ((y + kd) % 4) * 2 + (c + ke) % 2
    pick = ((lists_ref[...] == tile_id) & (s_col < len_ref[...])).astype(F32).astype(BF16)
    keys = ko_ref[...] + 1
    k_hi = (keys // 256).astype(F32).astype(BF16)
    k_lo = (keys % 256).astype(F32).astype(BF16)
    koff[...] = dot(k_hi, pick, 1, 1) * 256.0 + dot(k_lo, pick, 1, 1) - 1.0
    length = len_ref[...].astype(F32)
    inverse = 1.0 / length
    hi_t = dot(pick, k_hi, 1, 1) + 4.0 * length
    lo_t = dot(pick, k_lo, 1, 1)
    for h in range(2):
        gbuf[0, h, HALF:, :HALF] = lo_t[:, h * HALF:(h + 1) * HALF].astype(BF16)
        gbuf[0, h, HALF:, HALF:] = hi_t[:, h * HALF:(h + 1) * HALF].astype(BF16)

    loads["t"].wait()
    loads["ws"].wait()
    base[...] = dot(tv[...], wsv[...])

    lanes = lax.broadcasted_iota(jnp.int32, (512, 512), 1).astype(F32)

    def gather_tile(t, init=False):
        pattern = jnp.where(koff[:, t:t + 1] == lanes, 1.0, 0.0).astype(BF16)
        added = dot(pattern, sbuf[t].reshape(512, 512))
        acc[...] = added if init else acc[...] + added

    gather_tile(slot(0, 0, 0), True)
    first.wait(0, 0, 1, 0)
    first.wait(0, 0, 1, 1)
    gather_tile(slot(0, 0, 1))
    first.take(0, 3, 0)
    first.take(0, 1, 1)
    first.take(1, 0, 0)
    first.take(1, 0, 1)
    gather_tile(slot(1, 0, 0))
    first.take(0, 1, 0)
    first.take(0, 3, 1)
    gather_tile(slot(0, 3, 0))
    gather_tile(slot(0, 1, 0))
    for dy, h in ((3, 0), (1, 1)):
        first.take(1, dy, h)
    first.take(0, 2, 0)
    first.take(0, 2, 1)
    gather_tile(slot(0, 2, 0))
    for col, dy in ((1, 0), (0, 3), (0, 1), (0, 2)):
        first.wait(col, dy, 1, 0)
        first.wait(col, dy, 1, 1)
        gather_tile(slot(col, dy, 1))
    first.take(1, 1, 0)
    first.take(1, 3, 1)
    gather_tile(slot(1, 1, 0))
    gather_tile(slot(1, 3, 0))
    first.take(1, 2, 0)
    first.take(1, 2, 1)
    for dy in (1, 3):
        first.wait(1, dy, 1, 0)
        first.wait(1, dy, 1, 1)
        gather_tile(slot(1, dy, 1))
    gather_tile(slot(1, 2, 0))
    first.wait(1, 2, 1, 0)
    first.wait(1, 2, 1, 1)
    gather_tile(slot(1, 2, 1))

    loads["wm"].wait()
    loads["cot"].wait()
    second = Gather(gbuf, ssend2, srecv2)
    for h in range(2):
        part = pl.ds(h * HALF, HALF)
        mean = (acc[part, :] * inverse).astype(BF16)
        bbuf[part, :] = mean
        pre = base[part, :] + dot(mean, wmv[...])
        sig = jax.nn.sigmoid(pre)
        grad = cotv[part, :].astype(F32) * sig * (1.0 + pre * (1.0 - sig))
        gbuf[0, h, :HALF, :] = grad.astype(BF16)
        second.start(h)
        updv[part, :] = (tv[part, :].astype(F32) + pre * sig).astype(BF16)
    out_u = pltpu.make_async_copy(updv, upd_hbm, lsem.at[5])
    out_u.start()

    grads = gbuf[0, :, :HALF, :].reshape(512, 512)
    is_self = c == 0
    t_val, b_val = tv[...], bbuf[...]
    give[...] = dot(jnp.where(is_self, b_val, t_val), grads, 0, 0).astype(BF16)
    to_sib = remote(give, got, gsem.at[0], gsem.at[1], dev(flip=True))
    to_sib.start()
    sends.append(to_sib)
    base[...] = dot(jnp.where(is_self, t_val, b_val), grads, 0, 0)
    tgv[...] = (cotv[...].astype(F32) + dot(grads, wsv[...], 1, 1)).astype(BF16)
    out_t = pltpu.make_async_copy(tgv, tg_hbm, lsem.at[6])
    out_t.start()

    to_sib.wait_recv()
    wsend[...] = (base[...] + got[...].astype(F32)).astype(BF16).reshape(16, 32, 512)
    place = x * 4 + y
    w_in = []
    for i, (dx, dy) in enumerate(plane):
        peer = lax.rem(x + dx, XN) * 4 + lax.rem(y + dy, YN)
        cp = remote(wsend.at[peer], wrecv.at[i], wssem.at[i], wrsem.at[i], dev(dx, dy))
        cp.start()
        w_in.append(cp)
        sends.append(cp)

    sub = lax.broadcasted_iota(jnp.int32, (512, HALF), 0).astype(F32)

    def scatter_half(col, dy, core, h, init=False):
        t = slot(col, dy, core)
        mine = slot(col, (4 - dy) % 4, core)
        notes = gbuf[t, h, HALF:, :].astype(F32)[mine:mine + 1, :]
        hi = notes[:, HALF:]
        count = jnp.floor(hi * 0.25)
        key = notes[:, :HALF] + (hi - 4.0 * count) * 256.0 - 1.0
        pattern = jnp.where(key == sub, 1.0, 0.0).astype(BF16)
        added = dot(pattern, gbuf[t, h, :HALF, :]) * (1.0 / count[:, :1])
        acc[...] = added if init else acc[...] + added

    scatter_half(0, 0, 0, 0, True)
    scatter_half(0, 0, 0, 1)
    for h in range(2):
        second.wait(0, 0, 1, h)
        scatter_half(0, 0, 1, h)

    second.take(0, 3, 0)
    second.take(0, 1, 1)
    second.take(1, 0, 0)
    second.take(1, 0, 1)
    scatter_half(1, 0, 0, 0)
    scatter_half(1, 0, 0, 1)
    second.take(0, 1, 0)
    second.take(0, 3, 1)

    total = wsend[place].astype(F32)
    for i, cp in enumerate(w_in):
        cp.wait_recv()
        total = total + wrecv[i].astype(F32)
    zbuf[z] = total.astype(BF16)
    z_in = []
    for dz in range(1, ZN):
        cp = remote(zbuf.at[z], zbuf.at[z], zssem.at[dz], zrsem.at[z], dev(0, 0, dz))
        cp.start()
        sends.append(cp)

    for h in range(2):
        scatter_half(0, 3, 0, h)
        scatter_half(0, 1, 0, h)
    for dy, h in ((3, 0), (1, 1)):
        second.take(1, dy, h)
        scatter_half(1, dy, 0, h)
    second.take(0, 2, 0)
    second.take(0, 2, 1)

    for dz in range(1, ZN):
        peer = lax.rem(z + dz, ZN)
        remote(zbuf.at[peer], zbuf.at[peer], zssem.at[dz], zrsem.at[peer], dev(flip=True)).wait_recv()
    total = zbuf[0].astype(F32)
    for i in range(1, ZN):
        total = total + zbuf[i].astype(F32)
    wres[c, place] = total.astype(BF16)
    for i, (dx, dy) in enumerate(plane):
        cp = remote(wres.at[c, place], wres.at[c, place], assem.at[i], arsem.at[i], dev(dx, dy))
        cp.start()
        sends.append(cp)

    for h in range(2):
        scatter_half(0, 2, 0, h)
    for col, dy in ((1, 0), (0, 3), (0, 1), (0, 2)):
        for h in range(2):
            second.wait(col, dy, 1, h)
            scatter_half(col, dy, 1, h)
    second.take(1, 1, 0)
    second.take(1, 3, 1)
    second.take(1, 2, 0)
    second.take(1, 2, 1)
    for dy, h in ((1, 0), (3, 1), (2, 0), (2, 1)):
        scatter_half(1, dy, 0, h)
    for dy in (1, 3, 2):
        for h in range(2):
            second.wait(1, dy, 1, h)
            scatter_half(1, dy, 1, h)

    rsend[...] = acc[...].astype(BF16).reshape(16, 32, 512)
    r_in = []
    for i, (dxh, dz) in enumerate(rows):
        peer = lax.rem(lax.div(r, 8) + dxh, 2) * 8 + lax.rem(z + dz, ZN)
        cp = remote(rsend.at[peer], rrecv.at[i], rssem.at[i], rrsem.at[i], dev(2 * dxh, 0, dz))
        cp.start()
        r_in.append(cp)
        sends.append(cp)

    for i, (dx, dy) in enumerate(plane):
        peer = lax.rem(x + (XN - dx), XN) * 4 + lax.rem(y + (YN - dy), YN)
        remote(wres.at[c, peer], wres.at[c, peer], assem.at[i], arsem.at[i], dev(flip=True)).wait_recv()
    cross = remote(wres.at[c], wres.at[c], bssem, brsem, dev(flip=True))
    cross.start()
    sends.append(cross)

    total = rsend[r].astype(F32)
    for i, cp in enumerate(r_in):
        cp.wait_recv()
        total = total + rrecv[i].astype(F32)
    sg_ref[...] = dot(total.astype(BF16), wmv[...], 1, 1).astype(BF16)

    remote(wres.at[1 - c], wres.at[1 - c], bssem, brsem, dev(flip=True)).wait_recv()
    out_w = pltpu.make_async_copy(wres, w_out, lsem.at[7])
    out_w.start()
    for cp in sends:
        cp.wait_send()
    out_u.wait()
    out_t.wait()
    out_w.wait()


def local(
    source_table, target_table, message_weight, self_weight, tile_lists, key_offsets, list_lengths, cotangent
):
    any_spec = pl.BlockSpec(memory_space=pl.ANY)
    vmem = pl.BlockSpec(memory_space=pltpu.VMEM)
    dma = pltpu.SemaphoreType.DMA
    square = (512, 512)
    updated, target_gradient, source_gradient, weights = pl.pallas_call(
        kernel,
        out_shape=(
            jax.ShapeDtypeStruct(square, BF16),
            jax.ShapeDtypeStruct(square, BF16),
            jax.ShapeDtypeStruct((32, 512), BF16),
            jax.ShapeDtypeStruct((2, 16, 32, 512), BF16),
        ),
        in_specs=[any_spec, any_spec, any_spec, any_spec, vmem, vmem, vmem, any_spec],
        out_specs=(any_spec, any_spec, vmem, any_spec),
        scratch_shapes=[
            pltpu.VMEM((16, 2, HALF, 512), BF16),
            pltpu.VMEM((16, 2, HALF + EXTRA, 512), BF16),
            pltpu.VMEM(square, BF16),
            pltpu.VMEM(square, BF16),
            pltpu.VMEM(square, BF16),
            pltpu.VMEM(square, BF16),
            pltpu.VMEM(square, F32),
            pltpu.VMEM(square, F32),
            pltpu.VMEM(square, BF16),
            pltpu.VMEM(square, BF16),
            pltpu.VMEM(square, BF16),
            pltpu.VMEM((512, 16), F32),
            pltpu.VMEM(square, BF16),
            pltpu.VMEM(square, BF16),
            pltpu.VMEM((16, 32, 512), BF16),
            pltpu.VMEM((15, 32, 512), BF16),
            pltpu.VMEM((8, 32, 512), BF16),
            pltpu.VMEM((2, 16, 32, 512), BF16),
            pltpu.VMEM((16, 32, 512), BF16),
            pltpu.VMEM((15, 32, 512), BF16),
            dma((8,)),
            dma((30,)), dma((32,)),
            dma((30,)), dma((32,)),
            dma((2,)),
            dma((15,)), dma((15,)),
            dma((8,)), dma((8,)),
            dma((15,)), dma((15,)),
            dma(()), dma(()),
            dma((15,)), dma((15,)),
        ],
        compiler_params=pltpu.CompilerParams(
            collective_id=0, has_side_effects=True, vmem_limit_bytes=56 * 1024 * 1024
        ),
    )(
        source_table.reshape(2, HALF, 512), target_table, message_weight, self_weight, tile_lists, key_offsets,
        list_lengths.reshape(1, 1), cotangent,
    )
    weights = weights.reshape(2, 512, 512).astype(F32)
    self_gradient = weights[0] * 131072 ** (-0.5)
    message_gradient = weights[1] * 8192 ** (-0.5)
    return updated, target_gradient, source_gradient, self_gradient, message_gradient


def solution(mesh):
    placed = (
        P("blk", None),
        P(("row", "blk"), None),
        P(),
        P(),
        P(("row", "blk"), None),
        P(("row", "blk"), None),
        P(("row", "blk")),
        P(("row", "blk"), None),
    )
    return jax.shard_map(
        local,
        mesh=mesh,
        in_specs=placed,
        out_specs=(
            P(("row", "blk"), None),
            P(("row", "blk"), None),
            P(("blk", "row"), None),
            P(),
            P(),
        ),
        check_vma=False,
    )
```

time: 811 us -> 115 us (0.14)
  the two profiles are of different devices: /device:TPU:1 before, /device:TPU:10 now
where the time goes in v1:
time: 115 us; the launch traced here: 114 us
  Pallas kernels  106 us (92%)
  local copies, waits for them, and re-layouts  3.81 us (3%)
  other arithmetic  3.08 us (3%)
  between operations  1.31 us (1%)
    pallas_call x1, Pallas kernels, local(): pl.pallas_call(kernel, out_shape=(jax.ShapeDtypeStruct(square, BF16), jax...  106 us
    unnamed x10, local copies, waits for them, and re-layouts  3.81 us

profile of v1, /device:TPU:10, one launch (start us, length us, event | category | flops | bytes accessed | tf_op | source)
XLA Modules:
  0.0 114.4 jit_solution(15980311519202499168)
XLA Ops:
  1.3 1.6 %copy.13.ko_ref = s32[512,16]{1,0:T(8,128)} copy(s32[512,16]{0,1:T(8,128)} %param.13) | data formatting | bytes 65536 | tf_op args[5]
  2.9 106.2 %shard_map.119 = (bf16[512,512]{1,0:T(8,128)(2,1)}, bf16[512,512]{1,0:T(8,128)(2,1)}, bf16[32,512]{1,0:T(8,128)(2,1)}, bf16[2,16,32,512]{3,2,1,0:T(8,128)(2,1)}) custom-call(bf16[2,256,512]{2,1,0:T(8,128)(2,1)} %bitcast.7, bf16[512,512]{1,0:T(8,128)(2,1)} %t_hbm.1, bf16[512,512]{1,0:T(8,128)(2,1)} %wm_hbm.1, bf16[512,512]{1,0:T(8,128)(2,1)} %ws_hbm.1, ...), custom_call_target="tpu_custom_call" | custom-call | tf_op jit(solution)/shard_map/pallas_call | solution.py:334
  109.1 1.5 %convert_element_type.4 = f32[2,16,32,512]{3,2,1,0:T(8,128)S(1)} convert(bf16[2,16,32,512]{3,2,1,0:T(8,128)(2,1)} %get-tuple-element.12) | non-fusion elementwise | flops 524288 | bytes 3145728 | tf_op jit(solution)/shard_map/convert_element_type | solution.py:382
  110.6 0.0 copy-start.1
  110.6 0.0 copy-start
  110.6 1.6 %slice_multiply_fusion = (f32[1,16,32,512]{3,2,1,0:T(8,128)}, f32[1,16,32,512]{3,2,1,0:T(8,128)}) fusion(f32[2,16,32,512]{3,2,1,0:T(8,128)S(1)} %convert_element_type.4), kind=kLoop, calls=%fused_computation | loop fusion | flops 524288 | bytes 4194304 | tf_op jit(solution)/shard_map/mul | solution.py:384
  112.2 0.0 copy-start.2
  112.2 0.0 copy-done.1
  112.2 0.8 copy.18
  113.0 0.0 copy-done
  113.0 0.8 copy.19
  113.8 0.0 copy-done.2
  113.8 0.6 copy.20
Async XLA Ops:
  110.6 1.6 %copy-start.1 = (bf16[512,512]{1,0:T(8,128)(2,1)S(1)}, bf16[512,512]{1,0:T(8,128)(2,1)}, u32[]{:S(2)}) copy-start(bf16[512,512]{1,0:T(8,128)(2,1)} %get-tuple-element.20) | copy-start | bytes 1572868
  110.6 2.4 %copy-start = (bf16[512,512]{1,0:T(8,128)(2,1)S(1)}, bf16[512,512]{1,0:T(8,128)(2,1)}, u32[]{:S(2)}) copy-start(bf16[512,512]{1,0:T(8,128)(2,1)} %get-tuple-element.21) | copy-start | bytes 1572868
  112.2 1.6 %copy-start.2 = (bf16[32,512]{1,0:T(8,128)(2,1)S(1)}, bf16[32,512]{1,0:T(8,128)(2,1)}, u32[]{:S(2)}) copy-start(bf16[32,512]{1,0:T(8,128)(2,1)} %get-tuple-element.22) | copy-start | bytes 98308

commit v2 on v1

--- a/solution.py
+++ b/solution.py
@@ -9,7 +9,8 @@
 
 XN, YN, ZN = 4, 4, 8
 HALF = 256
-EXTRA = 16
+PIECES = 2
+WIDE = 512 // PIECES
 F32 = jnp.float32
 BF16 = jnp.bfloat16
 
@@ -25,9 +26,10 @@
 def kernel(
     s_hbm, t_hbm, wm_hbm, ws_hbm, lists_ref, ko_ref, len_ref, cot_hbm,
     upd_hbm, tg_hbm, sg_ref, w_out,
-    sbuf, gbuf, tv, cotv, wmv, wsv, acc, base, bbuf, updv, tgv, koff,
-    give, got, wsend, wrecv, zbuf, wres, rsend, rrecv,
-    lsem, ssend1, srecv1, ssend2, srecv2, gsem, wssem, wrsem, zssem, zrsem, assem, arsem, bssem, brsem, rssem, rrsem,
+    sbuf, gbuf, notes, links, scale, tv, cotv, wmv, wsv, acc, base, bbuf, updv, tgv, koff, terms,
+    give, got, wsend, wrecv, zbuf, wres, xsend, xrecv, dsend, drecv,
+    lsem, ssend1, srecv1, nssem, nrsem, ssend2, srecv2, gsem, wssem, wrsem, zssem, zrsem, assem, arsem, bssem, brsem,
+    xssem, xrsem, dssem, drsem,
 ):
     r = lax.axis_index("row")
     b = lax.axis_index("blk")
@@ -57,11 +59,9 @@
         loads[name].start()
 
     plane = [(dx, dy) for dx in range(XN) for dy in range(YN) if (dx, dy) != (0, 0)]
-    rows = [(dxh, dz) for dxh in range(2) for dz in range(ZN) if (dxh, dz) != (0, 0)]
     barrier = pltpu.get_barrier_semaphore()
-    partners = [dev(flip=True)] + [dev(dx, dy) for dx, dy in plane] + [
-        dev(2 * dxh, 0, dz) for dxh, dz in rows if (dxh, dz) != (1, 0)
-    ]
+    partners = [dev(flip=True)] + [dev(dx, dy) for dx, dy in plane]
+    partners += [dev(0, dy, flip=True) for dy in range(1, YN)] + [dev(dz=dz) for dz in range(1, ZN)]
     for to in partners:
         pl.semaphore_signal(barrier, inc=1, device_id=to, device_id_type=pl.DeviceIdType.MESH)
     pl.semaphore_wait(barrier, len(partners))
@@ -119,14 +119,17 @@
     keys = ko_ref[...] + 1
     k_hi = (keys // 256).astype(F32).astype(BF16)
     k_lo = (keys % 256).astype(F32).astype(BF16)
-    koff[...] = dot(k_hi, pick, 1, 1) * 256.0 + dot(k_lo, pick, 1, 1) - 1.0
+    koff[...] = dot(k_hi, pick, 0, 1) * 256.0 + dot(k_lo, pick, 0, 1) - 1.0
     length = len_ref[...].astype(F32)
     inverse = 1.0 / length
-    hi_t = dot(pick, k_hi, 1, 1) + 4.0 * length
-    lo_t = dot(pick, k_lo, 1, 1)
-    for h in range(2):
-        gbuf[0, h, HALF:, :HALF] = lo_t[:, h * HALF:(h + 1) * HALF].astype(BF16)
-        gbuf[0, h, HALF:, HALF:] = hi_t[:, h * HALF:(h + 1) * HALF].astype(BF16)
+    notes[0, :16] = dot(pick, k_lo).astype(BF16)
+    notes[0, 16:] = (dot(pick, k_hi) + 4.0 * length).astype(BF16)
+    note_in = []
+    for i, (dy, core) in enumerate([(dy, core) for dy in range(YN) for core in range(2) if (dy, core) != (0, 0)]):
+        to = slot(0, (4 - dy) % 4, core)
+        cp = remote(notes.at[0], notes.at[to], nssem.at[i], nrsem.at[to], dev(0, dy, flip=core == 1))
+        cp.start()
+        sends.append(cp)
 
     loads["t"].wait()
     loads["ws"].wait()
@@ -139,7 +142,22 @@
         added = dot(pattern, sbuf[t].reshape(512, 512))
         acc[...] = added if init else acc[...] + added
 
+    sub = lax.broadcasted_iota(jnp.int32, (512, 512), 0).astype(F32)
+
+    def link_tile(i):
+        dy, core = i // 2, i % 2
+        if i:
+            remote(notes.at[i], notes.at[i], nssem.at[0], nrsem.at[i], dev(flip=True)).wait_recv()
+        for col in range(2):
+            k = slot(col, (4 - dy) % 4, core)
+            hi = notes[i, 16:, :].astype(F32)[k:k + 1, :]
+            count = jnp.floor(hi * 0.25)
+            key = notes[i, :16, :].astype(F32)[k:k + 1, :] + (hi - 4.0 * count) * 256.0 - 1.0
+            links[i, col * 512:(col + 1) * 512, :] = jnp.where(key == sub, 1.0, 0.0).astype(BF16)
+        scale[i:i + 1, :] = 1.0 / count[:, :128]
+
     gather_tile(slot(0, 0, 0), True)
+    link_tile(0)
     first.wait(0, 0, 1, 0)
     first.wait(0, 0, 1, 1)
     gather_tile(slot(0, 0, 1))
@@ -152,11 +170,15 @@
     first.take(0, 3, 1)
     gather_tile(slot(0, 3, 0))
     gather_tile(slot(0, 1, 0))
+    for i in range(1, 4):
+        link_tile(i)
     for dy, h in ((3, 0), (1, 1)):
         first.take(1, dy, h)
     first.take(0, 2, 0)
     first.take(0, 2, 1)
     gather_tile(slot(0, 2, 0))
+    for i in range(4, 8):
+        link_tile(i)
     for col, dy in ((1, 0), (0, 3), (0, 1), (0, 2)):
         first.wait(col, dy, 1, 0)
         first.wait(col, dy, 1, 1)
@@ -178,21 +200,48 @@
 
     loads["wm"].wait()
     loads["cot"].wait()
-    second = Gather(gbuf, ssend2, srecv2)
+
+    def ring(f, i, h, to_i, to, n):
+        part = pl.ds(h * HALF, HALF)
+        k = (f * 8 + to_i) * 2 + h
+        cp = remote(gbuf.at[f, i, part], gbuf.at[f, to_i, part], ssend2.at[f * 14 + n], srecv2.at[k], to)
+        cp.start()
+        sends.append(cp)
+
+    def arrive(f, i, h):
+        part = pl.ds(h * HALF, HALF)
+        remote(
+            gbuf.at[f, i, part], gbuf.at[f, i, part], ssend2.at[0], srecv2.at[(f * 8 + i) * 2 + h], dev(flip=True)
+        ).wait_recv()
+
+    def own_out(f, h):
+        for n, dy in enumerate((1, 3) if h == 0 else (3, 1)):
+            ring(f, 0, h, (4 - dy) % 4 * 2, dev(0, dy), h * 3 + n)
+        ring(f, 0, h, 1, dev(flip=True), h * 3 + 2)
+
+    def take(f, dy, h):
+        arrive(f, dy * 2, h)
+        if (dy, h) == (3, 0):
+            ring(f, dy * 2, h, 4, dev(0, 1), 6)
+        if (dy, h) == (1, 1):
+            ring(f, dy * 2, h, 4, dev(0, 3), 7)
+        ring(f, dy * 2, h, dy * 2 + 1, dev(flip=True), 8 + (dy - 1) * 2 + h)
+
     for h in range(2):
         part = pl.ds(h * HALF, HALF)
         mean = (acc[part, :] * inverse).astype(BF16)
         bbuf[part, :] = mean
         pre = base[part, :] + dot(mean, wmv[...])
         sig = jax.nn.sigmoid(pre)
-        grad = cotv[part, :].astype(F32) * sig * (1.0 + pre * (1.0 - sig))
-        gbuf[0, h, :HALF, :] = grad.astype(BF16)
-        second.start(h)
+        grad = (cotv[part, :].astype(F32) * sig * (1.0 + pre * (1.0 - sig))).astype(BF16)
+        for f in range(PIECES):
+            gbuf[f, 0, part, :] = grad[:, f * WIDE:(f + 1) * WIDE]
+        own_out(0, h)
         updv[part, :] = (tv[part, :].astype(F32) + pre * sig).astype(BF16)
     out_u = pltpu.make_async_copy(updv, upd_hbm, lsem.at[5])
     out_u.start()
 
-    grads = gbuf[0, :, :HALF, :].reshape(512, 512)
+    grads = jnp.concatenate([gbuf[f, 0] for f in range(PIECES)], axis=1)
     is_self = c == 0
     t_val, b_val = tv[...], bbuf[...]
     give[...] = dot(jnp.where(is_self, b_val, t_val), grads, 0, 0).astype(BF16)
@@ -200,9 +249,6 @@
     to_sib.start()
     sends.append(to_sib)
     base[...] = dot(jnp.where(is_self, t_val, b_val), grads, 0, 0)
-    tgv[...] = (cotv[...].astype(F32) + dot(grads, wsv[...], 1, 1)).astype(BF16)
-    out_t = pltpu.make_async_copy(tgv, tg_hbm, lsem.at[6])
-    out_t.start()
 
     to_sib.wait_recv()
     wsend[...] = (base[...] + got[...].astype(F32)).astype(BF16).reshape(16, 32, 512)
@@ -215,91 +261,112 @@
         w_in.append(cp)
         sends.append(cp)
 
-    sub = lax.broadcasted_iota(jnp.int32, (512, HALF), 0).astype(F32)
-
-    def scatter_half(col, dy, core, h, init=False):
-        t = slot(col, dy, core)
-        mine = slot(col, (4 - dy) % 4, core)
-        notes = gbuf[t, h, HALF:, :].astype(F32)[mine:mine + 1, :]
-        hi = notes[:, HALF:]
-        count = jnp.floor(hi * 0.25)
-        key = notes[:, :HALF] + (hi - 4.0 * count) * 256.0 - 1.0
-        pattern = jnp.where(key == sub, 1.0, 0.0).astype(BF16)
-        added = dot(pattern, gbuf[t, h, :HALF, :]) * (1.0 / count[:, :1])
-        acc[...] = added if init else acc[...] + added
-
-    scatter_half(0, 0, 0, 0, True)
-    scatter_half(0, 0, 0, 1)
-    for h in range(2):
-        second.wait(0, 0, 1, h)
-        scatter_half(0, 0, 1, h)
-
-    second.take(0, 3, 0)
-    second.take(0, 1, 1)
-    second.take(1, 0, 0)
-    second.take(1, 0, 1)
-    scatter_half(1, 0, 0, 0)
-    scatter_half(1, 0, 0, 1)
-    second.take(0, 1, 0)
-    second.take(0, 3, 1)
-
-    total = wsend[place].astype(F32)
-    for i, cp in enumerate(w_in):
-        cp.wait_recv()
-        total = total + wrecv[i].astype(F32)
-    zbuf[z] = total.astype(BF16)
-    z_in = []
-    for dz in range(1, ZN):
-        cp = remote(zbuf.at[z], zbuf.at[z], zssem.at[dz], zrsem.at[z], dev(0, 0, dz))
-        cp.start()
-        sends.append(cp)
-
-    for h in range(2):
-        scatter_half(0, 3, 0, h)
-        scatter_half(0, 1, 0, h)
-    for dy, h in ((3, 0), (1, 1)):
-        second.take(1, dy, h)
-        scatter_half(1, dy, 0, h)
-    second.take(0, 2, 0)
-    second.take(0, 2, 1)
-
-    for dz in range(1, ZN):
-        peer = lax.rem(z + dz, ZN)
-        remote(zbuf.at[peer], zbuf.at[peer], zssem.at[dz], zrsem.at[peer], dev(flip=True)).wait_recv()
-    total = zbuf[0].astype(F32)
-    for i in range(1, ZN):
-        total = total + zbuf[i].astype(F32)
-    wres[c, place] = total.astype(BF16)
-    for i, (dx, dy) in enumerate(plane):
-        cp = remote(wres.at[c, place], wres.at[c, place], assem.at[i], arsem.at[i], dev(dx, dy))
-        cp.start()
-        sends.append(cp)
-
-    for h in range(2):
-        scatter_half(0, 2, 0, h)
-    for col, dy in ((1, 0), (0, 3), (0, 1), (0, 2)):
+    tgv[...] = (cotv[...].astype(F32) + dot(grads, wsv[...], 1, 1)).astype(BF16)
+    out_t = pltpu.make_async_copy(tgv, tg_hbm, lsem.at[6])
+    out_t.start()
+
+    def scatter(f, dy, core):
+        i = dy * 2 + core
+        added = dot(links[i], gbuf[f, i]) * scale[i:i + 1, :1]
+        terms[f] = added if i == 0 else terms[f] + added
+
+    def gather_piece(f):
+        scatter(f, 0, 0)
         for h in range(2):
-            second.wait(col, dy, 1, h)
-            scatter_half(col, dy, 1, h)
-    second.take(1, 1, 0)
-    second.take(1, 3, 1)
-    second.take(1, 2, 0)
-    second.take(1, 2, 1)
-    for dy, h in ((1, 0), (3, 1), (2, 0), (2, 1)):
-        scatter_half(1, dy, 0, h)
-    for dy in (1, 3, 2):
+            arrive(f, 1, h)
+        scatter(f, 0, 1)
+        take(f, 3, 0)
+        take(f, 1, 1)
+        take(f, 3, 1)
+        take(f, 1, 0)
+        if f + 1 < PIECES:
+            own_out(f + 1, 0)
+            own_out(f + 1, 1)
+        scatter(f, 3, 0)
+        scatter(f, 1, 0)
+        for i in (7, 3):
+            for h in range(2):
+                arrive(f, i, h)
+            scatter(f, i // 2, 1)
+        take(f, 2, 0)
+        take(f, 2, 1)
+        scatter(f, 2, 0)
         for h in range(2):
-            second.wait(1, dy, 1, h)
-            scatter_half(1, dy, 1, h)
-
-    rsend[...] = acc[...].astype(BF16).reshape(16, 32, 512)
-    r_in = []
-    for i, (dxh, dz) in enumerate(rows):
-        peer = lax.rem(lax.div(r, 8) + dxh, 2) * 8 + lax.rem(z + dz, ZN)
-        cp = remote(rsend.at[peer], rrecv.at[i], rssem.at[i], rrsem.at[i], dev(2 * dxh, 0, dz))
-        cp.start()
-        r_in.append(cp)
-        sends.append(cp)
+            arrive(f, 5, h)
+        scatter(f, 2, 1)
+
+    def x_out(f):
+        xsend[f] = terms[f].astype(BF16).reshape(2, 2, HALF, WIDE)
+        for dx in range(1, XN):
+            xh = lax.div(lax.rem(x + dx, XN), 2)
+            cp = remote(
+                xsend.at[f, dx % 2, xh], xrecv.at[f, dx - 1], xssem.at[f * 3 + dx - 1], xrsem.at[f * 3 + dx - 1], dev(dx)
+            )
+            cp.start()
+            sends.append(cp)
+
+    def z_out(f):
+        total = xsend[f, 0, lax.div(x, 2)].astype(F32)
+        for i in range(XN - 1):
+            remote(
+                xrecv.at[f, i], xrecv.at[f, i], xssem.at[0], xrsem.at[f * 3 + i], dev(flip=True)
+            ).wait_recv()
+            total = total + xrecv[f, i].astype(F32)
+        dsend[f] = total.astype(BF16).reshape(8, 32, WIDE)
+        for dz in range(1, ZN):
+            n = f * 7 + dz - 1
+            cp = remote(
+                dsend.at[f, lax.rem(z + dz, ZN)], drecv.at[f, dz - 1], dssem.at[n], drsem.at[n], dev(dz=dz)
+            )
+            cp.start()
+            sends.append(cp)
+
+    def finish(f):
+        total = dsend[f, z].astype(F32)
+        for i in range(ZN - 1):
+            remote(
+                drecv.at[f, i], drecv.at[f, i], dssem.at[0], drsem.at[f * 7 + i], dev(flip=True)
+            ).wait_recv()
+            total = total + drecv[f, i].astype(F32)
+        return dot(total.astype(BF16), wmv[:, f * WIDE:(f + 1) * WIDE], 1, 1)
+
+    def weights_z():
+        total = wsend[place].astype(F32)
+        for i, cp in enumerate(w_in):
+            cp.wait_recv()
+            total = total + wrecv[i].astype(F32)
+        zbuf[z] = total.astype(BF16)
+        for dz in range(1, ZN):
+            cp = remote(zbuf.at[z], zbuf.at[z], zssem.at[dz], zrsem.at[z], dev(0, 0, dz))
+            cp.start()
+            sends.append(cp)
+
+    def weights_out():
+        for dz in range(1, ZN):
+            peer = lax.rem(z + dz, ZN)
+            remote(zbuf.at[peer], zbuf.at[peer], zssem.at[dz], zrsem.at[peer], dev(flip=True)).wait_recv()
+        total = zbuf[0].astype(F32)
+        for i in range(1, ZN):
+            total = total + zbuf[i].astype(F32)
+        wres[c, place] = total.astype(BF16)
+        for i, (dx, dy) in enumerate(plane):
+            cp = remote(wres.at[c, place], wres.at[c, place], assem.at[i], arsem.at[i], dev(dx, dy))
+            cp.start()
+            sends.append(cp)
+
+    gather_piece(0)
+    x_out(0)
+    weights_z()
+    for f in range(1, PIECES):
+        gather_piece(f)
+        x_out(f)
+        z_out(f - 1)
+        if f == 1:
+            weights_out()
+    out = finish(0)
+    for f in range(1, PIECES - 1):
+        out = out + finish(f)
+    z_out(PIECES - 1)
 
     for i, (dx, dy) in enumerate(plane):
         peer = lax.rem(x + (XN - dx), XN) * 4 + lax.rem(y + (YN - dy), YN)
@@ -308,11 +375,7 @@
     cross.start()
     sends.append(cross)
 
-    total = rsend[r].astype(F32)
-    for i, cp in enumerate(r_in):
-        cp.wait_recv()
-        total = total + rrecv[i].astype(F32)
-    sg_ref[...] = dot(total.astype(BF16), wmv[...], 1, 1).astype(BF16)
+    sg_ref[...] = (out + finish(PIECES - 1)).astype(BF16)
 
     remote(wres.at[1 - c], wres.at[1 - c], bssem, brsem, dev(flip=True)).wait_recv()
     out_w = pltpu.make_async_copy(wres, w_out, lsem.at[7])
@@ -322,6 +385,15 @@
     out_u.wait()
     out_t.wait()
     out_w.wait()
+
+
+def place_outputs(upd, tg, sg, w, upd_out, tg_out, sg_out, self_out, message_out):
+    upd_out[...] = upd[...]
+    tg_out[...] = tg[...]
+    sg_out[...] = sg[...]
+    rows = w.shape[1] * 32
+    self_out[...] = w[0].reshape(rows, 512).astype(F32) * 131072 ** (-0.5)
+    message_out[...] = w[1].reshape(rows, 512).astype(F32) * 8192 ** (-0.5)
 
 
 def local(
@@ -343,7 +415,10 @@
         out_specs=(any_spec, any_spec, vmem, any_spec),
         scratch_shapes=[
             pltpu.VMEM((16, 2, HALF, 512), BF16),
-            pltpu.VMEM((16, 2, HALF + EXTRA, 512), BF16),
+            pltpu.VMEM((PIECES, 8, 512, WIDE), BF16),
+            pltpu.VMEM((8, 32, 512), BF16),
+            pltpu.VMEM((8, 1024, 512), BF16),
+            pltpu.VMEM((8, 128), F32),
             pltpu.VMEM(square, BF16),
             pltpu.VMEM(square, BF16),
             pltpu.VMEM(square, BF16),
@@ -354,35 +429,53 @@
             pltpu.VMEM(square, BF16),
             pltpu.VMEM(square, BF16),
             pltpu.VMEM((512, 16), F32),
+            pltpu.VMEM((PIECES, 1024, WIDE), F32),
             pltpu.VMEM(square, BF16),
             pltpu.VMEM(square, BF16),
             pltpu.VMEM((16, 32, 512), BF16),
             pltpu.VMEM((15, 32, 512), BF16),
             pltpu.VMEM((8, 32, 512), BF16),
             pltpu.VMEM((2, 16, 32, 512), BF16),
-            pltpu.VMEM((16, 32, 512), BF16),
-            pltpu.VMEM((15, 32, 512), BF16),
+            pltpu.VMEM((PIECES, 2, 2, HALF, WIDE), BF16),
+            pltpu.VMEM((PIECES, 3, HALF, WIDE), BF16),
+            pltpu.VMEM((PIECES, 8, 32, WIDE), BF16),
+            pltpu.VMEM((PIECES, 7, 32, WIDE), BF16),
             dma((8,)),
             dma((30,)), dma((32,)),
-            dma((30,)), dma((32,)),
+            dma((7,)), dma((8,)),
+            dma((14 * PIECES,)), dma((16 * PIECES,)),
             dma((2,)),
             dma((15,)), dma((15,)),
             dma((8,)), dma((8,)),
             dma((15,)), dma((15,)),
             dma(()), dma(()),
-            dma((15,)), dma((15,)),
+            dma((3 * PIECES,)), dma((3 * PIECES,)),
+            dma((7 * PIECES,)), dma((7 * PIECES,)),
         ],
         compiler_params=pltpu.CompilerParams(
             collective_id=0, has_side_effects=True, vmem_limit_bytes=56 * 1024 * 1024
         ),
     )(
-        source_table.reshape(2, HALF, 512), target_table, message_weight, self_weight, tile_lists, key_offsets,
+        source_table.reshape(2, HALF, 512), target_table, message_weight, self_weight, tile_lists, key_offsets.T,
         list_lengths.reshape(1, 1), cotangent,
     )
-    weights = weights.reshape(2, 512, 512).astype(F32)
-    self_gradient = weights[0] * 131072 ** (-0.5)
-    message_gradient = weights[1] * 8192 ** (-0.5)
-    return updated, target_gradient, source_gradient, self_gradient, message_gradient
+    steps = 4
+    rows = 512 // steps
+    wide = pl.BlockSpec((rows, 512), lambda i: (i, 0))
+    small = pl.BlockSpec((32, 512), lambda i: (0, 0))
+    return pl.pallas_call(
+        place_outputs,
+        grid=(steps,),
+        out_shape=(
+            jax.ShapeDtypeStruct(square, BF16),
+            jax.ShapeDtypeStruct(square, BF16),
+            jax.ShapeDtypeStruct((32, 512), BF16),
+            jax.ShapeDtypeStruct(square, F32),
+            jax.ShapeDtypeStruct(square, F32),
+        ),
+        in_specs=[wide, wide, small, pl.BlockSpec((2, rows // 32, 32, 512), lambda i: (0, i, 0, 0))],
+        out_specs=(wide, wide, small, wide, wide),
+    )(updated, target_gradient, source_gradient, weights)
 
 
 def solution(mesh):

time: 115 us -> 99.9 us (0.87)
  the two profiles are of different devices: /device:TPU:10 before, /device:TPU:1 now
where the time goes in v2:
time: 99.9 us; the launch traced here: 99.7 us
  Pallas kernels  98.4 us (98%)
  between operations  1.29 us (1%)
    pallas_call x1, Pallas kernels, local(): pl.pallas_call(kernel, out_shape=(jax.ShapeDtypeStruct(square, BF16), jax...  94.4 us
    pallas_call x1, Pallas kernels, local(): pl.pallas_call(place_outputs, grid=(steps,), out_shape=(jax.ShapeDtypeStr...  3.98 us

profile of v2, /device:TPU:1, one launch (start us, length us, event | category | flops | bytes accessed | tf_op | source)
XLA Modules:
  0.0 99.7 jit_solution(3241329537332729323)
XLA Ops:
  1.3 94.4 %shard_map.119 = (bf16[512,512]{1,0:T(8,128)(2,1)}, bf16[512,512]{1,0:T(8,128)(2,1)}, bf16[32,512]{1,0:T(8,128)(2,1)}, bf16[2,16,32,512]{3,2,1,0:T(8,128)(2,1)}) custom-call(bf16[2,256,512]{2,1,0:T(8,128)(2,1)} %bitcast.4, bf16[512,512]{1,0:T(8,128)(2,1)} %t_hbm.1, bf16[512,512]{1,0:T(8,128)(2,1)} %wm_hbm.1, bf16[512,512]{1,0:T(8,128)(2,1)} %ws_hbm.1, ...), custom_call_target="tpu_custom_call" | custom-call | tf_op jit(solution)/shard_map/pallas_call | solution.py:406
  95.7 4.0 %shard_map.120 = (bf16[512,512]{1,0:T(8,128)(2,1)}, bf16[512,512]{1,0:T(8,128)(2,1)}, bf16[32,512]{1,0:T(8,128)(2,1)}, f32[512,512]{1,0:T(8,128)}, f32[512,512]{1,0:T(8,128)}) custom-call(bf16[512,512]{1,0:T(8,128)(2,1)} %get-tuple-element.9.upd, bf16[512,512]{1,0:T(8,128)(2,1)} %get-tuple-element.10.tg, bf16[32,512]{1,0:T(8,128)(2,1)} %get-tuple-element.11.sg, ...), custom_call_target="tpu_custom_call" | custom-call | tf_op jit(solution)/shard_map/pallas_call | solution.py:466

commit v3 on v2

--- a/solution.py
+++ b/solution.py
@@ -27,7 +27,7 @@
     s_hbm, t_hbm, wm_hbm, ws_hbm, lists_ref, ko_ref, len_ref, cot_hbm,
     upd_hbm, tg_hbm, sg_ref, w_out,
     sbuf, gbuf, notes, links, scale, tv, cotv, wmv, wsv, acc, base, bbuf, updv, tgv, koff, terms,
-    give, got, wsend, wrecv, zbuf, wres, xsend, xrecv, dsend, drecv,
+    give, got, wsend, wrecv, ysend, yrecv, zbuf, wres, xsend, xrecv, dsend, drecv,
     lsem, ssend1, srecv1, nssem, nrsem, ssend2, srecv2, gsem, wssem, wrsem, zssem, zrsem, assem, arsem, bssem, brsem,
     xssem, xrsem, dssem, drsem,
 ):
@@ -68,47 +68,48 @@
 
     sends = []
 
-    class Gather:
-        def __init__(self, buf, ssem, rsem):
-            self.buf, self.ssem, self.rsem, self.n = buf, ssem, rsem, 0
-
-        def send(self, t, h, to_t, to):
-            cp = remote(
-                self.buf.at[t, h], self.buf.at[to_t, h], self.ssem.at[self.n], self.rsem.at[to_t * 2 + h], to
-            )
-            cp.start()
-            self.n += 1
-            sends.append(cp)
-
-        def start(self, h):
-            t = slot(0, 0, 0)
-            first = (1, 3) if h == 0 else (3, 1)
-            for dy in first:
-                self.send(t, h, slot(0, (4 - dy) % 4, 0), dev(0, dy))
-            self.send(t, h, slot(1, 0, 0), dev(1 if h == 0 else 3, 0))
-            self.send(t, h, slot(0, 0, 1), dev(flip=True))
-
-        def wait(self, col, dy, core, h):
-            t = slot(col, dy, core)
-            remote(
-                self.buf.at[t, h], self.buf.at[t, h], self.ssem.at[0], self.rsem.at[t * 2 + h], dev(flip=True)
-            ).wait_recv()
-
-        def take(self, col, dy, h):
-            self.wait(col, dy, 0, h)
-            t = slot(col, dy, 0)
-            if col == 0:
-                if (dy, h) == (3, 0):
-                    self.send(t, h, slot(0, 2, 0), dev(0, 1))
-                if (dy, h) == (1, 1):
-                    self.send(t, h, slot(0, 2, 0), dev(0, 3))
-                self.send(t, h, slot(1, dy, 0), dev(1 if h == 0 else 3, 0))
-            self.send(t, h, slot(col, dy, 1), dev(flip=True))
-
-    first = Gather(sbuf, ssend1, srecv1)
+    parity = lax.rem(z, 2)
+    made = [0]
+
+    def part_of(t, role):
+        base_row = 2 * parity if role < 2 else 2 - 2 * parity
+        return sbuf.at[t, base_row + role % 2]
+
+    def push(t, role, to_t, to_role, to):
+        cp = remote(part_of(t, role), part_of(to_t, role), ssend1.at[made[0]], srecv1.at[to_t * 4 + to_role], to)
+        cp.start()
+        made[0] += 1
+        sends.append(cp)
+
+    def got_part(col, dy, core, role):
+        t = slot(col, dy, core)
+        remote(part_of(t, role), part_of(t, role), ssend1.at[0], srecv1.at[t * 4 + role], dev(flip=True)).wait_recv()
+
+    def got_tile(col, dy):
+        for role in range(4):
+            got_part(col, dy, 1, role)
+
+    def fetch(col, dy, role):
+        got_part(col, dy, 0, role)
+        t = slot(col, dy, 0)
+        if col == 0 and dy == 3 and role in (0, 2):
+            push(t, role, slot(0, 2, 0), role, dev(0, 1))
+        if col == 0 and dy == 1 and role in (1, 3):
+            push(t, role, slot(0, 2, 0), role, dev(0, 3))
+        if role < 2 and (col, dy) not in ((0, 2), (1, 0)):
+            push(t, role, t, role + 2, dev(dz=ZN - 1 if role == 0 else 1))
+        if role < 2 and col == 0:
+            push(t, role, slot(1, dy, 0), role, dev(1 if role == 0 else 3))
+        push(t, role, slot(col, dy, 1), role, dev(flip=True))
+
     loads["s"].wait()
-    first.start(0)
-    first.start(1)
+    for role in (0, 1):
+        push(0, role, slot(0, 3, 0), role, dev(0, 1))
+        push(0, 1 - role, slot(0, 1, 0), 1 - role, dev(0, 3))
+        push(0, 2 * role, slot(1, 0, 0), 2 * role, dev(1))
+        push(0, 2 * role + 1, slot(1, 0, 0), 2 * role + 1, dev(3))
+    for role in range(4):
+        push(0, role, slot(0, 0, 1), role, dev(flip=True))
 
     k_row = lax.broadcasted_iota(jnp.int32, (16, 16), 0)
     s_col = lax.broadcasted_iota(jnp.int32, (16, 16), 1)
@@ -158,44 +159,56 @@
 
     gather_tile(slot(0, 0, 0), True)
     link_tile(0)
-    first.wait(0, 0, 1, 0)
-    first.wait(0, 0, 1, 1)
+    fetch(0, 3, 0)
+    fetch(0, 1, 1)
+    fetch(1, 0, 0)
+    fetch(1, 0, 1)
+    got_tile(0, 0)
     gather_tile(slot(0, 0, 1))
-    first.take(0, 3, 0)
-    first.take(0, 1, 1)
-    first.take(1, 0, 0)
-    first.take(1, 0, 1)
+    fetch(0, 3, 1)
+    fetch(0, 1, 0)
+    fetch(1, 0, 2)
+    fetch(1, 0, 3)
     gather_tile(slot(1, 0, 0))
-    first.take(0, 1, 0)
-    first.take(0, 3, 1)
+    fetch(0, 3, 2)
+    fetch(0, 1, 3)
+    fetch(0, 2, 0)
+    fetch(0, 2, 1)
+    fetch(1, 3, 0)
+    fetch(1, 1, 1)
+    link_tile(1)
+    link_tile(2)
+    fetch(0, 1, 2)
+    fetch(0, 3, 3)
+    gather_tile(slot(0, 1, 0))
+    fetch(1, 1, 0)
+    fetch(1, 3, 1)
     gather_tile(slot(0, 3, 0))
-    gather_tile(slot(0, 1, 0))
-    for i in range(1, 4):
-        link_tile(i)
-    for dy, h in ((3, 0), (1, 1)):
-        first.take(1, dy, h)
-    first.take(0, 2, 0)
-    first.take(0, 2, 1)
+    fetch(0, 2, 2)
+    fetch(0, 2, 3)
+    fetch(1, 3, 2)
+    fetch(1, 1, 3)
     gather_tile(slot(0, 2, 0))
-    for i in range(4, 8):
-        link_tile(i)
-    for col, dy in ((1, 0), (0, 3), (0, 1), (0, 2)):
-        first.wait(col, dy, 1, 0)
-        first.wait(col, dy, 1, 1)
-        gather_tile(slot(col, dy, 1))
-    first.take(1, 1, 0)
-    first.take(1, 3, 1)
+    fetch(1, 2, 0)
+    fetch(1, 2, 1)
+    got_tile(1, 0)
+    gather_tile(slot(1, 0, 1))
+    fetch(1, 1, 2)
+    fetch(1, 3, 3)
+    for dy in (1, 3, 2):
+        got_tile(0, dy)
+        gather_tile(slot(0, dy, 1))
     gather_tile(slot(1, 1, 0))
     gather_tile(slot(1, 3, 0))
-    first.take(1, 2, 0)
-    first.take(1, 2, 1)
+    for i in range(3, 8):
+        link_tile(i)
+    fetch(1, 2, 2)
+    fetch(1, 2, 3)
     for dy in (1, 3):
-        first.wait(1, dy, 1, 0)
-        first.wait(1, dy, 1, 1)
+        got_tile(1, dy)
         gather_tile(slot(1, dy, 1))
     gather_tile(slot(1, 2, 0))
-    first.wait(1, 2, 1, 0)
-    first.wait(1, 2, 1, 1)
+    got_tile(1, 2)
     gather_tile(slot(1, 2, 1))
 
     loads["wm"].wait()
@@ -253,12 +266,12 @@
     to_sib.wait_recv()
     wsend[...] = (base[...] + got[...].astype(F32)).astype(BF16).reshape(16, 32, 512)
     place = x * 4 + y
-    w_in = []
-    for i, (dx, dy) in enumerate(plane):
-        peer = lax.rem(x + dx, XN) * 4 + lax.rem(y + dy, YN)
-        cp = remote(wsend.at[peer], wrecv.at[i], wssem.at[i], wrsem.at[i], dev(dx, dy))
+    for dx in range(1, XN):
+        to_x = lax.rem(x + dx, XN)
+        cp = remote(
+            wsend.at[pl.ds(to_x * 4, 4)], wrecv.at[pl.ds(dx * 4 - 4, 4)], wssem.at[dx - 1], wrsem.at[dx - 1], dev(dx)
+        )
         cp.start()
-        w_in.append(cp)
         sends.append(cp)
 
     tgv[...] = (cotv[...].astype(F32) + dot(grads, wsv[...], 1, 1)).astype(BF16)
@@ -284,6 +297,8 @@
             own_out(f + 1, 1)
         scatter(f, 3, 0)
         scatter(f, 1, 0)
+        if f == 0:
+            weights_y()
         for i in (7, 3):
             for h in range(2):
                 arrive(f, i, h)
@@ -330,11 +345,25 @@
             total = total + drecv[f, i].astype(F32)
         return dot(total.astype(BF16), wmv[:, f * WIDE:(f + 1) * WIDE], 1, 1)
 
+    def weights_y():
+        total = wsend[pl.ds(x * 4, 4)].astype(F32)
+        for i in range(XN - 1):
+            got_x = wrecv.at[pl.ds(i * 4, 4)]
+            remote(got_x, got_x, wssem.at[0], wrsem.at[i], dev(flip=True)).wait_recv()
+            total = total + got_x[...].astype(F32)
+        ysend[...] = total.astype(BF16)
+        for dy in range(1, YN):
+            cp = remote(
+                ysend.at[lax.rem(y + dy, YN)], yrecv.at[dy - 1], wssem.at[2 + dy], wrsem.at[2 + dy], dev(0, dy)
+            )
+            cp.start()
+            sends.append(cp)
+
     def weights_z():
-        total = wsend[place].astype(F32)
-        for i, cp in enumerate(w_in):
-            cp.wait_recv()
-            total = total + wrecv[i].astype(F32)
+        total = ysend[y].astype(F32)
+        for i in range(YN - 1):
+            remote(yrecv.at[i], yrecv.at[i], wssem.at[0], wrsem.at[3 + i], dev(flip=True)).wait_recv()
+            total = total + yrecv[i].astype(F32)
         zbuf[z] = total.astype(BF16)
         for dz in range(1, ZN):
             cp = remote(zbuf.at[z], zbuf.at[z], zssem.at[dz], zrsem.at[z], dev(0, 0, dz))
@@ -414,7 +443,7 @@
         in_specs=[any_spec, any_spec, any_spec, any_spec, vmem, vmem, vmem, any_spec],
         out_specs=(any_spec, any_spec, vmem, any_spec),
         scratch_shapes=[
-            pltpu.VMEM((16, 2, HALF, 512), BF16),
+            pltpu.VMEM((16, 4, 128, 512), BF16),
             pltpu.VMEM((PIECES, 8, 512, WIDE), BF16),
             pltpu.VMEM((8, 32, 512), BF16),
             pltpu.VMEM((8, 1024, 512), BF16),
@@ -433,7 +462,9 @@
             pltpu.VMEM(square, BF16),
             pltpu.VMEM(square, BF16),
             pltpu.VMEM((16, 32, 512), BF16),
-            pltpu.VMEM((15, 32, 512), BF16),
+            pltpu.VMEM((12, 32, 512), BF16),
+            pltpu.VMEM((4, 32, 512), BF16),
+            pltpu.VMEM((3, 32, 512), BF16),
             pltpu.VMEM((8, 32, 512), BF16),
             pltpu.VMEM((2, 16, 32, 512), BF16),
             pltpu.VMEM((PIECES, 2, 2, HALF, WIDE), BF16),
@@ -441,11 +472,11 @@
             pltpu.VMEM((PIECES, 8, 32, WIDE), BF16),
             pltpu.VMEM((PIECES, 7, 32, WIDE), BF16),
             dma((8,)),
-            dma((30,)), dma((32,)),
+            dma((60,)), dma((64,)),
             dma((7,)), dma((8,)),
             dma((14 * PIECES,)), dma((16 * PIECES,)),
             dma((2,)),
-            dma((15,)), dma((15,)),
+            dma((6,)), dma((6,)),
             dma((8,)), dma((8,)),
             dma((15,)), dma((15,)),
             dma(()), dma(()),
@@ -456,7 +487,7 @@
             collective_id=0, has_side_effects=True, vmem_limit_bytes=56 * 1024 * 1024
         ),
     )(
-        source_table.reshape(2, HALF, 512), target_table, message_weight, self_weight, tile_lists, key_offsets.T,
+        source_table.reshape(4, 128, 512), target_table, message_weight, self_weight, tile_lists, key_offsets.T,
         list_lengths.reshape(1, 1), cotangent,
     )
     steps = 4

time: 99.9 us -> 92.2 us (0.923)
  Pallas kernels: 98.4 us -> 90.7 us
    pallas_call x1, Pallas kernels: 94.4 us -> 86.7 us  [local(): pl.pallas_call(kernel, out_shape=(jax.ShapeDtypeStruct(square, BF16), jax...]
where the time goes in v3:
time: 92.2 us; the launch traced here: 92 us
  Pallas kernels  90.7 us (98%)
  between operations  1.29 us (1%)
    pallas_call x1, Pallas kernels, local(): pl.pallas_call(kernel, out_shape=(jax.ShapeDtypeStruct(square, BF16), jax...  86.7 us
    pallas_call x1, Pallas kernels, local(): pl.pallas_call(place_outputs, grid=(steps,), out_shape=(jax.ShapeDtypeStr...  3.98 us

profile of v3, /device:TPU:1, one launch (start us, length us, event | category | flops | bytes accessed | tf_op | source)
XLA Modules:
  0.0 92.0 jit_solution(2022341532605660539)
XLA Ops:
  1.3 86.7 %shard_map.119 = (bf16[512,512]{1,0:T(8,128)(2,1)}, bf16[512,512]{1,0:T(8,128)(2,1)}, bf16[32,512]{1,0:T(8,128)(2,1)}, bf16[2,16,32,512]{3,2,1,0:T(8,128)(2,1)}) custom-call(bf16[4,128,512]{2,1,0:T(8,128)(2,1)} %bitcast.4, bf16[512,512]{1,0:T(8,128)(2,1)} %t_hbm.1, bf16[512,512]{1,0:T(8,128)(2,1)} %wm_hbm.1, bf16[512,512]{1,0:T(8,128)(2,1)} %ws_hbm.1, ...), custom_call_target="tpu_custom_call" | custom-call | tf_op jit(solution)/shard_map/pallas_call | solution.py:435
  88.0 4.0 %shard_map.120 = (bf16[512,512]{1,0:T(8,128)(2,1)}, bf16[512,512]{1,0:T(8,128)(2,1)}, bf16[32,512]{1,0:T(8,128)(2,1)}, f32[512,512]{1,0:T(8,128)}, f32[512,512]{1,0:T(8,128)}) custom-call(bf16[512,512]{1,0:T(8,128)(2,1)} %get-tuple-element.9.upd, bf16[512,512]{1,0:T(8,128)(2,1)} %get-tuple-element.10.tg, bf16[32,512]{1,0:T(8,128)(2,1)} %get-tuple-element.11.sg, ...), custom_call_target="tpu_custom_call" | custom-call | tf_op jit(solution)/shard_map/pallas_call | solution.py:497

commit v4 on v3

--- a/solution.py
+++ b/solution.py
@@ -25,11 +25,11 @@
 
 def kernel(
     s_hbm, t_hbm, wm_hbm, ws_hbm, lists_ref, ko_ref, len_ref, cot_hbm,
-    upd_hbm, tg_hbm, sg_ref, w_out,
-    sbuf, gbuf, notes, links, scale, tv, cotv, wmv, wsv, acc, base, bbuf, updv, tgv, koff, terms,
+    updv, tgv, sg_ref, self_ref, message_ref,
+    sbuf, gbuf, nsend, notes, links, scale, tv, cotv, wmv, wsv, acc, base, bbuf, koff, terms,
     give, got, wsend, wrecv, ysend, yrecv, zbuf, wres, xsend, xrecv, dsend, drecv,
     lsem, ssend1, srecv1, nssem, nrsem, ssend2, srecv2, gsem, wssem, wrsem, zssem, zrsem, assem, arsem, bssem, brsem,
-    xssem, xrsem, dssem, drsem,
+    xssem, xrsem, dssem, drsem, near_sem, far_sem,
 ):
     r = lax.axis_index("row")
     b = lax.axis_index("blk")
@@ -59,14 +59,22 @@
         loads[name].start()
 
     plane = [(dx, dy) for dx in range(XN) for dy in range(YN) if (dx, dy) != (0, 0)]
-    barrier = pltpu.get_barrier_semaphore()
-    partners = [dev(flip=True)] + [dev(dx, dy) for dx, dy in plane]
-    partners += [dev(0, dy, flip=True) for dy in range(1, YN)] + [dev(dz=dz) for dz in range(1, ZN)]
-    for to in partners:
-        pl.semaphore_signal(barrier, inc=1, device_id=to, device_id_type=pl.DeviceIdType.MESH)
-    pl.semaphore_wait(barrier, len(partners))
+    nearest = [dev(flip=True), dev(1), dev(3), dev(0, 1), dev(0, 3), dev(dz=1), dev(dz=ZN - 1)]
+
+    def meet(sem, others):
+        for to in others:
+            pl.semaphore_signal(sem, inc=1, device_id=to, device_id_type=pl.DeviceIdType.MESH)
+        pl.semaphore_wait(sem, len(others))
+
+    meet(pltpu.get_barrier_semaphore(), nearest)
 
     sends = []
+
+    def settle():
+        for cp in sends:
+            cp.wait_send()
+        sends.clear()
+
 
     parity = lax.rem(z, 2)
     made = [0]
@@ -85,9 +93,23 @@
         t = slot(col, dy, core)
         remote(part_of(t, role), part_of(t, role), ssend1.at[0], srecv1.at[t * 4 + role], dev(flip=True)).wait_recv()
 
+    def half_of(t, pair):
+        return sbuf.at[t, pl.ds(2 * parity if pair == 0 else 2 - 2 * parity, 2)]
+
+    def push_half(t, to_t, pair):
+        half = half_of(t, pair)
+        cp = remote(half, half_of(to_t, pair), ssend1.at[made[0]], srecv1.at[to_t * 4 + 2 * pair], dev(flip=True))
+        cp.start()
+        made[0] += 1
+        sends.append(cp)
+
     def got_tile(col, dy):
-        for role in range(4):
-            got_part(col, dy, 1, role)
+        t = slot(col, dy, 1)
+        for pair in range(2):
+            half = half_of(t, pair)
+            remote(half, half, ssend1.at[0], srecv1.at[t * 4 + 2 * pair], dev(flip=True)).wait_recv()
+
+    here = set()
 
     def fetch(col, dy, role):
         got_part(col, dy, 0, role)
@@ -100,7 +122,9 @@
             push(t, role, t, role + 2, dev(dz=ZN - 1 if role == 0 else 1))
         if role < 2 and col == 0:
             push(t, role, slot(1, dy, 0), role, dev(1 if role == 0 else 3))
-        push(t, role, slot(col, dy, 1), role, dev(flip=True))
+        here.add((t, role))
+        if (t, role ^ 1) in here:
+            push_half(t, slot(col, dy, 1), role // 2)
 
     loads["s"].wait()
     for role in (0, 1):
@@ -108,8 +132,8 @@
         push(0, 1 - role, slot(0, 1, 0), 1 - role, dev(0, 3))
         push(0, 2 * role, slot(1, 0, 0), 2 * role, dev(1))
         push(0, 2 * role + 1, slot(1, 0, 0), 2 * role + 1, dev(3))
-    for role in range(4):
-        push(0, role, slot(0, 0, 1), role, dev(flip=True))
+    for pair in range(2):
+        push_half(0, slot(0, 0, 1), pair)
 
     k_row = lax.broadcasted_iota(jnp.int32, (16, 16), 0)
     s_col = lax.broadcasted_iota(jnp.int32, (16, 16), 1)
@@ -123,12 +147,17 @@
     koff[...] = dot(k_hi, pick, 0, 1) * 256.0 + dot(k_lo, pick, 0, 1) - 1.0
     length = len_ref[...].astype(F32)
     inverse = 1.0 / length
-    notes[0, :16] = dot(pick, k_lo).astype(BF16)
-    notes[0, 16:] = (dot(pick, k_hi) + 4.0 * length).astype(BF16)
-    note_in = []
-    for i, (dy, core) in enumerate([(dy, core) for dy in range(YN) for core in range(2) if (dy, core) != (0, 0)]):
+    meet(near_sem, nearest)
+    meet(far_sem, [dev(2), dev(0, 2), dev(dz=2), dev(dz=ZN - 2)])
+    keys_t = dot(pick, k_hi) * 256.0 + dot(pick, k_lo) - 1.0
+    for i in range(8):
+        nsend[i, 0:1, :] = keys_t[i:i + 1, :]
+        nsend[i, 1:2, :] = keys_t[8 + i:9 + i, :]
+        nsend[i, 2:3, :] = jnp.broadcast_to(inverse, (1, 512))
+    for i in range(1, 8):
+        dy, core = i // 2, i % 2
         to = slot(0, (4 - dy) % 4, core)
-        cp = remote(notes.at[0], notes.at[to], nssem.at[i], nrsem.at[to], dev(0, dy, flip=core == 1))
+        cp = remote(nsend.at[i], notes.at[to], nssem.at[i - 1], nrsem.at[to], dev(0, dy, flip=core == 1))
         cp.start()
         sends.append(cp)
 
@@ -146,16 +175,12 @@
     sub = lax.broadcasted_iota(jnp.int32, (512, 512), 0).astype(F32)
 
     def link_tile(i):
-        dy, core = i // 2, i % 2
         if i:
             remote(notes.at[i], notes.at[i], nssem.at[0], nrsem.at[i], dev(flip=True)).wait_recv()
+        note = nsend if i == 0 else notes
         for col in range(2):
-            k = slot(col, (4 - dy) % 4, core)
-            hi = notes[i, 16:, :].astype(F32)[k:k + 1, :]
-            count = jnp.floor(hi * 0.25)
-            key = notes[i, :16, :].astype(F32)[k:k + 1, :] + (hi - 4.0 * count) * 256.0 - 1.0
-            links[i, col * 512:(col + 1) * 512, :] = jnp.where(key == sub, 1.0, 0.0).astype(BF16)
-        scale[i:i + 1, :] = 1.0 / count[:, :128]
+            links[i, col * 512:(col + 1) * 512, :] = jnp.where(note[i, col:col + 1, :] == sub, 1.0, 0.0).astype(BF16)
+        scale[i:i + 1, :] = note[i, 2:3, :128]
 
     gather_tile(slot(0, 0, 0), True)
     link_tile(0)
@@ -228,9 +253,10 @@
         ).wait_recv()
 
     def own_out(f, h):
-        for n, dy in enumerate((1, 3) if h == 0 else (3, 1)):
-            ring(f, 0, h, (4 - dy) % 4 * 2, dev(0, dy), h * 3 + n)
-        ring(f, 0, h, 1, dev(flip=True), h * 3 + 2)
+        outs = ((1, 0),) if h == 0 else ((3, 1), (3, 0), (1, 1))
+        for dy, half in outs:
+            ring(f, 0, half, (4 - dy) % 4 * 2, dev(0, dy), half * 2 + dy // 2)
+        ring(f, 0, h, 1, dev(flip=True), 4 + h)
 
     def take(f, dy, h):
         arrive(f, dy * 2, h)
@@ -251,8 +277,6 @@
             gbuf[f, 0, part, :] = grad[:, f * WIDE:(f + 1) * WIDE]
         own_out(0, h)
         updv[part, :] = (tv[part, :].astype(F32) + pre * sig).astype(BF16)
-    out_u = pltpu.make_async_copy(updv, upd_hbm, lsem.at[5])
-    out_u.start()
 
     grads = jnp.concatenate([gbuf[f, 0] for f in range(PIECES)], axis=1)
     is_self = c == 0
@@ -275,8 +299,6 @@
         sends.append(cp)
 
     tgv[...] = (cotv[...].astype(F32) + dot(grads, wsv[...], 1, 1)).astype(BF16)
-    out_t = pltpu.make_async_copy(tgv, tg_hbm, lsem.at[6])
-    out_t.start()
 
     def scatter(f, dy, core):
         i = dy * 2 + core
@@ -298,6 +320,8 @@
         scatter(f, 3, 0)
         scatter(f, 1, 0)
         if f == 0:
+            for cp in old:
+                cp.wait_send()
             weights_y()
         for i in (7, 3):
             for h in range(2):
@@ -383,6 +407,8 @@
             cp.start()
             sends.append(cp)
 
+    old = list(sends)
+    sends.clear()
     gather_piece(0)
     x_out(0)
     weights_z()
@@ -391,6 +417,7 @@
         x_out(f)
         z_out(f - 1)
         if f == 1:
+            settle()
             weights_out()
     out = finish(0)
     for f in range(1, PIECES - 1):
@@ -406,23 +433,27 @@
 
     sg_ref[...] = (out + finish(PIECES - 1)).astype(BF16)
 
+    def self_done():
+        self_ref[...] = wres[0].reshape(512, 512).astype(F32) * 131072 ** (-0.5)
+
+    def message_done():
+        message_ref[...] = wres[1].reshape(512, 512).astype(F32) * 8192 ** (-0.5)
+
+    pl.when(c == 0)(self_done)
+    pl.when(c == 1)(message_done)
     remote(wres.at[1 - c], wres.at[1 - c], bssem, brsem, dev(flip=True)).wait_recv()
-    out_w = pltpu.make_async_copy(wres, w_out, lsem.at[7])
-    out_w.start()
-    for cp in sends:
-        cp.wait_send()
-    out_u.wait()
-    out_t.wait()
-    out_w.wait()
-
-
-def place_outputs(upd, tg, sg, w, upd_out, tg_out, sg_out, self_out, message_out):
-    upd_out[...] = upd[...]
-    tg_out[...] = tg[...]
-    sg_out[...] = sg[...]
-    rows = w.shape[1] * 32
-    self_out[...] = w[0].reshape(rows, 512).astype(F32) * 131072 ** (-0.5)
-    message_out[...] = w[1].reshape(rows, 512).astype(F32) * 8192 ** (-0.5)
+    pl.when(c == 1)(self_done)
+    pl.when(c == 0)(message_done)
+    settle()
+
+
+def place_outputs(*refs):
+    count = len(refs) // 2
+    copies = [pltpu.make_async_copy(refs[i], refs[count + i], refs[-1].at[i]) for i in range(count)]
+    for cp in copies:
+        cp.start()
+    for cp in copies:
+        cp.wait()
 
 
 def local(
@@ -432,20 +463,17 @@
     vmem = pl.BlockSpec(memory_space=pltpu.VMEM)
     dma = pltpu.SemaphoreType.DMA
     square = (512, 512)
-    updated, target_gradient, source_gradient, weights = pl.pallas_call(
+    shapes = ((square, BF16), (square, BF16), ((32, 512), BF16), (square, F32), (square, F32))
+    held = pl.pallas_call(
         kernel,
-        out_shape=(
-            jax.ShapeDtypeStruct(square, BF16),
-            jax.ShapeDtypeStruct(square, BF16),
-            jax.ShapeDtypeStruct((32, 512), BF16),
-            jax.ShapeDtypeStruct((2, 16, 32, 512), BF16),
-        ),
+        out_shape=tuple(pltpu.VMEM(*shape) for shape in shapes),
         in_specs=[any_spec, any_spec, any_spec, any_spec, vmem, vmem, vmem, any_spec],
-        out_specs=(any_spec, any_spec, vmem, any_spec),
+        out_specs=(vmem,) * 5,
         scratch_shapes=[
             pltpu.VMEM((16, 4, 128, 512), BF16),
             pltpu.VMEM((PIECES, 8, 512, WIDE), BF16),
-            pltpu.VMEM((8, 32, 512), BF16),
+            pltpu.VMEM((8, 8, 512), F32),
+            pltpu.VMEM((8, 8, 512), F32),
             pltpu.VMEM((8, 1024, 512), BF16),
             pltpu.VMEM((8, 128), F32),
             pltpu.VMEM(square, BF16),
@@ -454,8 +482,6 @@
             pltpu.VMEM(square, BF16),
             pltpu.VMEM(square, F32),
             pltpu.VMEM(square, F32),
-            pltpu.VMEM(square, BF16),
-            pltpu.VMEM(square, BF16),
             pltpu.VMEM(square, BF16),
             pltpu.VMEM((512, 16), F32),
             pltpu.VMEM((PIECES, 1024, WIDE), F32),
@@ -471,8 +497,8 @@
             pltpu.VMEM((PIECES, 3, HALF, WIDE), BF16),
             pltpu.VMEM((PIECES, 8, 32, WIDE), BF16),
             pltpu.VMEM((PIECES, 7, 32, WIDE), BF16),
-            dma((8,)),
-            dma((60,)), dma((64,)),
+            dma((5,)),
+            dma((44,)), dma((64,)),
             dma((7,)), dma((8,)),
             dma((14 * PIECES,)), dma((16 * PIECES,)),
             dma((2,)),
@@ -482,6 +508,7 @@
             dma(()), dma(()),
             dma((3 * PIECES,)), dma((3 * PIECES,)),
             dma((7 * PIECES,)), dma((7 * PIECES,)),
+            pltpu.SemaphoreType.REGULAR, pltpu.SemaphoreType.REGULAR,
         ],
         compiler_params=pltpu.CompilerParams(
             collective_id=0, has_side_effects=True, vmem_limit_bytes=56 * 1024 * 1024
@@ -490,23 +517,13 @@
         source_table.reshape(4, 128, 512), target_table, message_weight, self_weight, tile_lists, key_offsets.T,
         list_lengths.reshape(1, 1), cotangent,
     )
-    steps = 4
-    rows = 512 // steps
-    wide = pl.BlockSpec((rows, 512), lambda i: (i, 0))
-    small = pl.BlockSpec((32, 512), lambda i: (0, 0))
     return pl.pallas_call(
         place_outputs,
-        grid=(steps,),
-        out_shape=(
-            jax.ShapeDtypeStruct(square, BF16),
-            jax.ShapeDtypeStruct(square, BF16),
-            jax.ShapeDtypeStruct((32, 512), BF16),
-            jax.ShapeDtypeStruct(square, F32),
-            jax.ShapeDtypeStruct(square, F32),
-        ),
-        in_specs=[wide, wide, small, pl.BlockSpec((2, rows // 32, 32, 512), lambda i: (0, i, 0, 0))],
-        out_specs=(wide, wide, small, wide, wide),
-    )(updated, target_gradient, source_gradient, weights)
+        out_shape=tuple(jax.ShapeDtypeStruct(*shape) for shape in shapes),
+        in_specs=[vmem] * 5,
+        out_specs=(any_spec,) * 5,
+        scratch_shapes=[dma((5,))],
+    )(*[pltpu.with_memory_space_constraint(one, pltpu.VMEM) for one in held])
 
 
 def solution(mesh):

time: 92.2 us -> 86.2 us (0.935)
  Pallas kernels: 90.7 us -> 84.6 us
    pallas_call x2, Pallas kernels: 90.7 us -> 84.6 us  [the longest x1 82.9 us: local(): pl.pallas_call(kernel, out_shape=tuple((pltpu.VMEM(*shape) for shape in s...]
where the time goes in v4:
time: 86.2 us; the launch traced here: 86 us
  Pallas kernels  84.6 us (98%)
  between operations  1.45 us (2%)
    pallas_call x1, Pallas kernels, local(): pl.pallas_call(kernel, out_shape=tuple((pltpu.VMEM(*shape) for shape in s...  82.9 us

profile of v4, /device:TPU:1, one launch (start us, length us, event | category | flops | bytes accessed | tf_op | source)
XLA Modules:
  0.0 86.0 jit_solution(8942445521116610357)
XLA Ops:
  1.3 82.9 %shard_map.119 = (bf16[512,512]{1,0:T(8,128)(2,1)S(1)}, bf16[512,512]{1,0:T(8,128)(2,1)S(1)}, bf16[32,512]{1,0:T(8,128)(2,1)S(1)}, f32[512,512]{1,0:T(8,128)S(1)}, f32[512,512]{1,0:T(8,128)S(1)}) custom-call(bf16[4,128,512]{2,1,0:T(8,128)(2,1)} %bitcast.4, bf16[512,512]{1,0:T(8,128)(2,1)} %t_hbm.1, bf16[512,512]{1,0:T(8,128)(2,1)} %wm_hbm.1, ...), custom_call_target="tpu_custom_call" | custom-call | tf_op jit(solution)/shard_map/pallas_call | solution.py:467
  84.2 1.7 %shard_map.120 = (bf16[512,512]{1,0:T(8,128)(2,1)}, bf16[512,512]{1,0:T(8,128)(2,1)}, bf16[32,512]{1,0:T(8,128)(2,1)}, f32[512,512]{1,0:T(8,128)}, f32[512,512]{1,0:T(8,128)}) custom-call(bf16[512,512]{1,0:T(8,128)(2,1)S(1)} %get-tuple-element.10.refs_0_, bf16[512,512]{1,0:T(8,128)(2,1)S(1)} %get-tuple-element.11.refs_1_, ...), custom_call_target="tpu_custom_call" | custom-call | tf_op jit(solution)/shard_map/pallas_call | solution.py:520

commit v5 on v4

--- a/solution.py
+++ b/solution.py
@@ -276,7 +276,7 @@
         for f in range(PIECES):
             gbuf[f, 0, part, :] = grad[:, f * WIDE:(f + 1) * WIDE]
         own_out(0, h)
-        updv[part, :] = (tv[part, :].astype(F32) + pre * sig).astype(BF16)
+        acc[part, :] = pre * sig
 
     grads = jnp.concatenate([gbuf[f, 0] for f in range(PIECES)], axis=1)
     is_self = c == 0
@@ -298,41 +298,10 @@
         cp.start()
         sends.append(cp)
 
-    tgv[...] = (cotv[...].astype(F32) + dot(grads, wsv[...], 1, 1)).astype(BF16)
-
     def scatter(f, dy, core):
         i = dy * 2 + core
         added = dot(links[i], gbuf[f, i]) * scale[i:i + 1, :1]
         terms[f] = added if i == 0 else terms[f] + added
-
-    def gather_piece(f):
-        scatter(f, 0, 0)
-        for h in range(2):
-            arrive(f, 1, h)
-        scatter(f, 0, 1)
-        take(f, 3, 0)
-        take(f, 1, 1)
-        take(f, 3, 1)
-        take(f, 1, 0)
-        if f + 1 < PIECES:
-            own_out(f + 1, 0)
-            own_out(f + 1, 1)
-        scatter(f, 3, 0)
-        scatter(f, 1, 0)
-        if f == 0:
-            for cp in old:
-                cp.wait_send()
-            weights_y()
-        for i in (7, 3):
-            for h in range(2):
-                arrive(f, i, h)
-            scatter(f, i // 2, 1)
-        take(f, 2, 0)
-        take(f, 2, 1)
-        scatter(f, 2, 0)
-        for h in range(2):
-            arrive(f, 5, h)
-        scatter(f, 2, 1)
 
     def x_out(f):
         xsend[f] = terms[f].astype(BF16).reshape(2, 2, HALF, WIDE)
@@ -407,31 +376,69 @@
             cp.start()
             sends.append(cp)
 
+    def sibling(f, dy):
+        for h in range(2):
+            arrive(f, dy * 2 + 1, h)
+        scatter(f, dy, 1)
+
     old = list(sends)
     sends.clear()
-    gather_piece(0)
+    take(0, 3, 0)
+    take(0, 1, 1)
+    tgv[...] = (cotv[...].astype(F32) + dot(grads, wsv[...], 1, 1)).astype(BF16)
+    take(0, 3, 1)
+    take(0, 1, 0)
+    own_out(1, 0)
+    own_out(1, 1)
+    scatter(0, 0, 0)
+    sibling(0, 0)
+    scatter(0, 3, 0)
+    scatter(0, 1, 0)
+    take(0, 2, 0)
+    take(0, 2, 1)
+    sibling(0, 3)
+    sibling(0, 1)
+    weights_y()
+    scatter(0, 2, 0)
+    sibling(0, 2)
     x_out(0)
+    take(1, 3, 0)
+    take(1, 1, 1)
+    scatter(1, 0, 0)
+    sibling(1, 0)
     weights_z()
-    for f in range(1, PIECES):
-        gather_piece(f)
-        x_out(f)
-        z_out(f - 1)
-        if f == 1:
-            settle()
-            weights_out()
+    take(1, 3, 1)
+    take(1, 1, 0)
+    scatter(1, 3, 0)
+    scatter(1, 1, 0)
+    take(1, 2, 0)
+    take(1, 2, 1)
+    sibling(1, 3)
+    sibling(1, 1)
+    scatter(1, 2, 0)
+    sibling(1, 2)
+    x_out(1)
+    for cp in old:
+        cp.wait_send()
+    updv[...] = (tv[...].astype(F32) + acc[...]).astype(BF16)
+    z_out(0)
+    weights_out()
     out = finish(0)
-    for f in range(1, PIECES - 1):
-        out = out + finish(f)
-    z_out(PIECES - 1)
-
-    for i, (dx, dy) in enumerate(plane):
-        peer = lax.rem(x + (XN - dx), XN) * 4 + lax.rem(y + (YN - dy), YN)
-        remote(wres.at[c, peer], wres.at[c, peer], assem.at[i], arsem.at[i], dev(flip=True)).wait_recv()
-    cross = remote(wres.at[c], wres.at[c], bssem, brsem, dev(flip=True))
-    cross.start()
-    sends.append(cross)
-
-    sg_ref[...] = (out + finish(PIECES - 1)).astype(BF16)
+    z_out(1)
+    settle()
+
+    for dx in (0, 1, 3, 2):
+        for dy in range(YN):
+            if (dx, dy) != (0, 0):
+                i = plane.index((dx, dy))
+                peer = lax.rem(x + (XN - dx), XN) * 4 + lax.rem(y + (YN - dy), YN)
+                remote(wres.at[c, peer], wres.at[c, peer], assem.at[i], arsem.at[i], dev(flip=True)).wait_recv()
+        part = wres.at[c, pl.ds(lax.rem(x + (XN - dx), XN) * 4, 4)]
+        cp = remote(part, part, bssem.at[dx], brsem.at[dx], dev(flip=True))
+        cp.start()
+        sends.append(cp)
+
+    sg_ref[...] = (out + finish(1)).astype(BF16)
 
     def self_done():
         self_ref[...] = wres[0].reshape(512, 512).astype(F32) * 131072 ** (-0.5)
@@ -441,7 +448,9 @@
 
     pl.when(c == 0)(self_done)
     pl.when(c == 1)(message_done)
-    remote(wres.at[1 - c], wres.at[1 - c], bssem, brsem, dev(flip=True)).wait_recv()
+    for dx in range(XN):
+        part = wres.at[1 - c, pl.ds(lax.rem(x + (XN - dx), XN) * 4, 4)]
+        remote(part, part, bssem.at[dx], brsem.at[dx], dev(flip=True)).wait_recv()
     pl.when(c == 1)(self_done)
     pl.when(c == 0)(message_done)
     settle()
@@ -505,7 +514,7 @@
             dma((6,)), dma((6,)),
             dma((8,)), dma((8,)),
             dma((15,)), dma((15,)),
-            dma(()), dma(()),
+            dma((4,)), dma((4,)),
             dma((3 * PIECES,)), dma((3 * PIECES,)),
             dma((7 * PIECES,)), dma((7 * PIECES,)),
             pltpu.SemaphoreType.REGULAR, pltpu.SemaphoreType.REGULAR,

time: 86.2 us -> 81.1 us (0.941)
  Pallas kernels: 84.6 us -> 79.5 us
    pallas_call x1, Pallas kernels: 82.9 us -> 77.8 us  [local(): pl.pallas_call(kernel, out_shape=tuple((pltpu.VMEM(*shape) for shape in s...]
where the time goes in v5:
time: 81.1 us; the launch traced here: 81 us
  Pallas kernels  79.5 us (98%)
  between operations  1.45 us (2%)
    pallas_call x1, Pallas kernels, local(): pl.pallas_call(kernel, out_shape=tuple((pltpu.VMEM(*shape) for shape in s...  77.8 us
    pallas_call x1, Pallas kernels, local(): pl.pallas_call(place_outputs, out_shape=tuple((jax.ShapeDtypeStruct(*shap...  1.72 us

profile of v5, /device:TPU:1, one launch (start us, length us, event | category | flops | bytes accessed | tf_op | source)
XLA Modules:
  0.0 81.0 jit_solution(7566629112563348608)
XLA Ops:
  1.3 77.8 %shard_map.119 = (bf16[512,512]{1,0:T(8,128)(2,1)S(1)}, bf16[512,512]{1,0:T(8,128)(2,1)S(1)}, bf16[32,512]{1,0:T(8,128)(2,1)S(1)}, f32[512,512]{1,0:T(8,128)S(1)}, f32[512,512]{1,0:T(8,128)S(1)}) custom-call(bf16[4,128,512]{2,1,0:T(8,128)(2,1)} %bitcast.4, bf16[512,512]{1,0:T(8,128)(2,1)} %t_hbm.1, bf16[512,512]{1,0:T(8,128)(2,1)} %wm_hbm.1, ...), custom_call_target="tpu_custom_call" | custom-call | tf_op jit(solution)/shard_map/pallas_call | solution.py:476
  79.1 1.7 %shard_map.120 = (bf16[512,512]{1,0:T(8,128)(2,1)}, bf16[512,512]{1,0:T(8,128)(2,1)}, bf16[32,512]{1,0:T(8,128)(2,1)}, f32[512,512]{1,0:T(8,128)}, f32[512,512]{1,0:T(8,128)}) custom-call(bf16[512,512]{1,0:T(8,128)(2,1)S(1)} %get-tuple-element.10.refs_0_, bf16[512,512]{1,0:T(8,128)(2,1)S(1)} %get-tuple-element.11.refs_1_, ...), custom_call_target="tpu_custom_call" | custom-call | tf_op jit(solution)/shard_map/pallas_call | solution.py:529

commit v6 on v5

--- a/solution.py
+++ b/solution.py
@@ -61,12 +61,15 @@
     plane = [(dx, dy) for dx in range(XN) for dy in range(YN) if (dx, dy) != (0, 0)]
     nearest = [dev(flip=True), dev(1), dev(3), dev(0, 1), dev(0, 3), dev(dz=1), dev(dz=ZN - 1)]
 
-    def meet(sem, others):
+    second = [dev(2), dev(0, 2), dev(dz=2), dev(dz=ZN - 2)]
+
+    def greet(sem, others):
         for to in others:
             pl.semaphore_signal(sem, inc=1, device_id=to, device_id_type=pl.DeviceIdType.MESH)
-        pl.semaphore_wait(sem, len(others))
-
-    meet(pltpu.get_barrier_semaphore(), nearest)
+
+    barrier = pltpu.get_barrier_semaphore()
+    greet(barrier, nearest)
+    pl.semaphore_wait(barrier, len(nearest))
 
     sends = []
 
@@ -147,8 +150,39 @@
     koff[...] = dot(k_hi, pick, 0, 1) * 256.0 + dot(k_lo, pick, 0, 1) - 1.0
     length = len_ref[...].astype(F32)
     inverse = 1.0 / length
-    meet(near_sem, nearest)
-    meet(far_sem, [dev(2), dev(0, 2), dev(dz=2), dev(dz=ZN - 2)])
+    greet(near_sem, nearest)
+
+    lanes = lax.broadcasted_iota(jnp.int32, (512, 512), 1).astype(F32)
+
+    def gather_tile(t, init=False):
+        pattern = jnp.where(koff[:, t:t + 1] == lanes, 1.0, 0.0).astype(BF16)
+        added = dot(pattern, sbuf[t].reshape(512, 512))
+        acc[...] = added if init else acc[...] + added
+
+    sub = lax.broadcasted_iota(jnp.int32, (512, 512), 0).astype(F32)
+
+    def link_tile(i):
+        if i:
+            remote(notes.at[i], notes.at[i], nssem.at[0], nrsem.at[i], dev(flip=True)).wait_recv()
+        note = nsend if i == 0 else notes
+        for col in range(2):
+            links[i, col * 512:(col + 1) * 512, :] = jnp.where(note[i, col:col + 1, :] == sub, 1.0, 0.0).astype(BF16)
+        scale[i:i + 1, :] = note[i, 2:3, :128]
+
+    gather_tile(slot(0, 0, 0), True)
+    fetch(0, 3, 0)
+    fetch(0, 1, 1)
+    fetch(1, 0, 0)
+    fetch(1, 0, 1)
+    pl.semaphore_wait(near_sem, len(nearest))
+    greet(far_sem, second)
+    got_tile(0, 0)
+    gather_tile(slot(0, 0, 1))
+    fetch(0, 3, 1)
+    fetch(0, 1, 0)
+    fetch(1, 0, 2)
+    fetch(1, 0, 3)
+    pl.semaphore_wait(far_sem, len(second))
     keys_t = dot(pick, k_hi) * 256.0 + dot(pick, k_lo) - 1.0
     for i in range(8):
         nsend[i, 0:1, :] = keys_t[i:i + 1, :]
@@ -161,48 +195,17 @@
         cp.start()
         sends.append(cp)
 
-    loads["t"].wait()
-    loads["ws"].wait()
-    base[...] = dot(tv[...], wsv[...])
-
-    lanes = lax.broadcasted_iota(jnp.int32, (512, 512), 1).astype(F32)
-
-    def gather_tile(t, init=False):
-        pattern = jnp.where(koff[:, t:t + 1] == lanes, 1.0, 0.0).astype(BF16)
-        added = dot(pattern, sbuf[t].reshape(512, 512))
-        acc[...] = added if init else acc[...] + added
-
-    sub = lax.broadcasted_iota(jnp.int32, (512, 512), 0).astype(F32)
-
-    def link_tile(i):
-        if i:
-            remote(notes.at[i], notes.at[i], nssem.at[0], nrsem.at[i], dev(flip=True)).wait_recv()
-        note = nsend if i == 0 else notes
-        for col in range(2):
-            links[i, col * 512:(col + 1) * 512, :] = jnp.where(note[i, col:col + 1, :] == sub, 1.0, 0.0).astype(BF16)
-        scale[i:i + 1, :] = note[i, 2:3, :128]
-
-    gather_tile(slot(0, 0, 0), True)
-    link_tile(0)
-    fetch(0, 3, 0)
-    fetch(0, 1, 1)
-    fetch(1, 0, 0)
-    fetch(1, 0, 1)
-    got_tile(0, 0)
-    gather_tile(slot(0, 0, 1))
-    fetch(0, 3, 1)
-    fetch(0, 1, 0)
-    fetch(1, 0, 2)
-    fetch(1, 0, 3)
-    gather_tile(slot(1, 0, 0))
     fetch(0, 3, 2)
     fetch(0, 1, 3)
     fetch(0, 2, 0)
     fetch(0, 2, 1)
     fetch(1, 3, 0)
     fetch(1, 1, 1)
-    link_tile(1)
-    link_tile(2)
+    gather_tile(slot(1, 0, 0))
+    loads["t"].wait()
+    loads["ws"].wait()
+    base[...] = dot(tv[...], wsv[...])
+
     fetch(0, 1, 2)
     fetch(0, 3, 3)
     gather_tile(slot(0, 1, 0))
@@ -218,6 +221,8 @@
     fetch(1, 2, 1)
     got_tile(1, 0)
     gather_tile(slot(1, 0, 1))
+    link_tile(0)
+    link_tile(1)
     fetch(1, 1, 2)
     fetch(1, 3, 3)
     for dy in (1, 3, 2):
@@ -225,7 +230,7 @@
         gather_tile(slot(0, dy, 1))
     gather_tile(slot(1, 1, 0))
     gather_tile(slot(1, 3, 0))
-    for i in range(3, 8):
+    for i in range(2, 8):
         link_tile(i)
     fetch(1, 2, 2)
     fetch(1, 2, 3)
@@ -398,10 +403,10 @@
     take(0, 2, 1)
     sibling(0, 3)
     sibling(0, 1)
-    weights_y()
     scatter(0, 2, 0)
     sibling(0, 2)
     x_out(0)
+    weights_y()
     take(1, 3, 0)
     take(1, 1, 1)
     scatter(1, 0, 0)
@@ -423,8 +428,8 @@
     updv[...] = (tv[...].astype(F32) + acc[...]).astype(BF16)
     z_out(0)
     weights_out()
+    z_out(1)
     out = finish(0)
-    z_out(1)
     settle()
 
     for dx in (0, 1, 3, 2):

time: 81.1 us -> 81.2 us (level)
  no operation moved by 1% of the time
where the time goes in v6:
time: 81.2 us; the launch traced here: 81 us
  Pallas kernels  79.5 us (98%)
  between operations  1.45 us (2%)
    pallas_call x1, Pallas kernels, local(): pl.pallas_call(kernel, out_shape=tuple((pltpu.VMEM(*shape) for shape in s...  77.8 us
    pallas_call x1, Pallas kernels, local(): pl.pallas_call(place_outputs, out_shape=tuple((jax.ShapeDtypeStruct(*shap...  1.72 us

profile of v6, /device:TPU:1, one launch (start us, length us, event | category | flops | bytes accessed | tf_op | source)
XLA Modules:
  0.0 81.0 jit_solution(6496918739244633326)
XLA Ops:
  1.3 77.8 %shard_map.119 = (bf16[512,512]{1,0:T(8,128)(2,1)S(1)}, bf16[512,512]{1,0:T(8,128)(2,1)S(1)}, bf16[32,512]{1,0:T(8,128)(2,1)S(1)}, f32[512,512]{1,0:T(8,128)S(1)}, f32[512,512]{1,0:T(8,128)S(1)}) custom-call(bf16[4,128,512]{2,1,0:T(8,128)(2,1)} %bitcast.4, bf16[512,512]{1,0:T(8,128)(2,1)} %t_hbm.1, bf16[512,512]{1,0:T(8,128)(2,1)} %wm_hbm.1, ...), custom_call_target="tpu_custom_call" | custom-call | tf_op jit(solution)/shard_map/pallas_call | solution.py:481
  79.1 1.7 %shard_map.120 = (bf16[512,512]{1,0:T(8,128)(2,1)}, bf16[512,512]{1,0:T(8,128)(2,1)}, bf16[32,512]{1,0:T(8,128)(2,1)}, f32[512,512]{1,0:T(8,128)}, f32[512,512]{1,0:T(8,128)}) custom-call(bf16[512,512]{1,0:T(8,128)(2,1)S(1)} %get-tuple-element.10.refs_0_, bf16[512,512]{1,0:T(8,128)(2,1)S(1)} %get-tuple-element.11.refs_1_, ...), custom_call_target="tpu_custom_call" | custom-call | tf_op jit(solution)/shard_map/pallas_call | solution.py:534
